TPU v7x, 32 devices: a whole 2x2x4 slice. The times are simulated.
32 devices in a mesh: seq: 8 (over z, x), tensor: 4 (over y, core).
Axes of the slice: x: 2, y: 2, z: 4, core: 2. Of those that a mesh axis runs over, the one named last changes fastest.
Arguments:
- latents: bfloat16 [1024, 2560], P('seq'), may hold values from -6 to 6
- levels: int32 [8], P('seq'), may hold values from 0 to 999
- head_slot: int32 [1], replicated, may hold values from 0 to 7
- fresh_noise: bfloat16 [128, 2560], P(None, 'tensor'), may hold values from -6 to 6
- ada_weight: bfloat16 [256, 3, 2560], P(None, None, 'tensor'), may hold values from -0.375 to 0.375
- qkv_weight: bfloat16 [2560, 3, 1536], P(None, None, 'tensor'), may hold values from -0.125 to 0.125
- q_gain: float32 [128], replicated, may hold values from 0.5 to 2.5
- k_gain: float32 [128], replicated, may hold values from 0.5 to 2.5
- out_weight: bfloat16 [1536, 2560], P('tensor'), may hold values from -0.15625 to 0.15625
Outputs:
- window: bfloat16 [1024, 2560], P('seq', 'tensor')
- clean: bfloat16 [128, 2560], P('seq', 'tensor')
All inputs are finite; a program needn't handle non-finite values.
Results may differ from a plain program's by a relative error of at most 0.0053.
Values may be sent and summed in bfloat16 or wider, within the bound.
A program may use at most 64 MiB of HBM per device.

v0:
```python
import functools
import math

import jax
import jax.numpy as jnp
from jax import lax
from jax.experimental import pallas as pl
from jax.experimental.pallas import tpu as pltpu
from jax.sharding import PartitionSpec as P

F32 = jnp.float32
BF16 = jnp.bfloat16
EPS = 1e-06


def dot(a, b):
    return jnp.dot(a, b, preferred_element_type=F32)


def dot_t(a, b):
    return lax.dot_general(a, b, (((1,), (1,)), ((), ())), preferred_element_type=F32)


def kernel(
    n, parts, slab, clean_rows,
    head_hbm, level_hbm, q_gain_hbm, k_gain_hbm, noise_hbm, lat_hbm, ada_hbm, qkv_hbm, out_hbm,
    updated_ref,
    head_ref, level_ref, q_gain_ref, k_gain_ref, noise, lat, ada, wqkv, wout, normed, hidden, mods, gates, lat_rows, kv, queries, q_rows,
    acc, totals, attended,
    load_sem, mod_send, mod_recv, gate_send, gate_recv, row_send, row_recv,
    kv_send, kv_recv, q_send, q_recv, w_send, w_recv, att_send, att_recv,
):
    me = lax.axis_index("seq")
    part = lax.axis_index("tensor")
    pair = 2
    side = lax.rem(me, pair)
    rows, width = lat.shape
    columns = updated_ref.shape[1]
    head_size = q_gain_ref.shape[1]
    heads = queries.shape[1] // head_size

    def remote(src, dst, send, recv, axis, target):
        return pltpu.make_async_remote_copy(
            src_ref=src, dst_ref=dst, send_sem=send, recv_sem=recv,
            device_id={axis: target}, device_id_type=pl.DeviceIdType.MESH,
        )

    loads = [
        pltpu.make_async_copy(ada_hbm, ada, load_sem.at[0]),
        pltpu.make_async_copy(lat_hbm, lat, load_sem.at[1]),
        pltpu.make_async_copy(qkv_hbm.at[1], wqkv.at[1], load_sem.at[2]),
        pltpu.make_async_copy(qkv_hbm.at[2], wqkv.at[2], load_sem.at[3]),
        pltpu.make_async_copy(qkv_hbm.at[0], wqkv.at[0], load_sem.at[4]),
        pltpu.make_async_copy(
            out_hbm.at[:, pl.ds(pl.multiple_of(part * columns, 128), columns)],
            wout.at[part], load_sem.at[5],
        ),
        pltpu.make_async_copy(noise_hbm, noise, load_sem.at[6]),
    ]
    small = [
        pltpu.make_async_copy(source, held, load_sem.at[7 + index])
        for index, (source, held) in enumerate((
            (level_hbm, level_ref), (head_hbm, head_ref),
            (q_gain_hbm, q_gain_ref), (k_gain_hbm, k_gain_ref),
        ))
    ]
    for load in small:
        load.start()
    for load in loads:
        load.start()

    barrier = pltpu.get_barrier_semaphore()
    for step in range(1, parts):
        pl.semaphore_signal(
            barrier, inc=1, device_id={"tensor": lax.rem(part + step, parts)},
            device_id_type=pl.DeviceIdType.MESH,
        )

    @pl.loop(1, n)
    def _(step):
        pl.semaphore_signal(
            barrier, inc=1, device_id={"seq": lax.rem(me + step, n)},
            device_id_type=pl.DeviceIdType.MESH,
        )

    for load in small:
        load.wait()
    half_width = ada.shape[1] // 2
    order = lax.broadcasted_iota(jnp.int32, (16, half_width), 1).astype(F32)
    angles = level_ref[0].astype(F32) * jnp.exp(-math.log(10000.0) * order / half_width)
    waves = jnp.concatenate([jnp.cos(angles), jnp.sin(angles)], axis=1)
    emb = (waves * (1.0 / (1.0 + jnp.exp(-waves)))).astype(BF16)
    loads[0].wait()
    for j in range(2):
        mods[part, j : j + 1, :] = dot(emb, ada[j])[0:1]
    gates[me] = dot(emb, ada[2])[0:1]

    pl.semaphore_wait(barrier, n - 1 + parts - 1)

    def mod_copy(slot, target):
        return remote(
            mods.at[slot], mods.at[slot], mod_send.at[target], mod_recv.at[slot], "tensor", target
        )

    for step in range(1, parts):
        mod_copy(part, lax.rem(part + step, parts)).start()


    def slab_of(device):
        return pl.multiple_of((device * clean_rows) // slab * slab, slab)

    first_column = pl.multiple_of(part * columns, 128)

    def gate_copy(slot, target):
        return remote(
            gates.at[slot], gates.at[slot], gate_send.at[target], gate_recv.at[slot], "seq", target
        )

    def row_copy(slot, target):
        return remote(
            lat_hbm.at[pl.ds(slab_of(target), slab), pl.ds(first_column, columns)],
            lat_rows.at[slot], row_send.at[target], row_recv.at[slot], "seq", target,
        )

    def w_copy(slot, target):
        at = pl.ds(pl.multiple_of(target * columns, 128), columns)
        return remote(
            out_hbm.at[:, at], wout.at[slot], w_send.at[target], w_recv.at[slot], "tensor", target
        )

    @pl.loop(1, n)
    def _(step):
        target = lax.rem(me + step, n)
        gate_copy(me, target).start()
        row_copy(me, target).start()

    for step in range(1, parts):
        w_copy(part, lax.rem(part + step, parts)).start()

    loads[1].wait()
    own_slab = slab_of(me)
    lat_rows[me] = lat[pl.ds(own_slab, slab), pl.ds(first_column, columns)]

    tile = 16

    @pl.loop(0, rows // tile)
    def _(index):
        at = pl.ds(pl.multiple_of(index * tile, tile), tile)
        states = lat[at, :].astype(F32)
        centered = states - jnp.mean(states, axis=-1, keepdims=True)
        variance = jnp.mean(centered * centered, axis=-1, keepdims=True)
        normed[at, :] = centered * lax.rsqrt(variance + EPS)

    for step in range(1, parts):
        mod_copy(lax.rem(part + step, parts), part).wait_recv()
    for index in range(parts):
        at = slice(index * columns, (index + 1) * columns)
        hidden[:, at] = (
            normed[:, at] * (1.0 + mods[index, 1:2, :]) + mods[index, 0:1, :]
        ).astype(BF16)

    def scaled(matrix, gain, factor):
        power = jnp.mean(matrix * matrix, axis=-1, keepdims=True)
        return (matrix * lax.rsqrt(power + EPS) * gain * factor).astype(BF16)

    def kv_copy(kind, slot, way, target):
        return remote(
            kv.at[slot, kind], kv.at[slot, kind],
            kv_send.at[kind, way, slot], kv_recv.at[kind, slot], "seq", target,
        )

    def onward(kind, slot, way, act):
        target = (me - pair, me + pair, me + 1 - 2 * side)[way]
        there = (target >= 0, target < n, None)[way]
        run = functools.partial(act, kind, slot, way, target)
        if there is None:
            run()
        else:
            pl.when(there)(run)

    def start(kind, slot, way, target):
        kv_copy(kind, slot, way, target).start()

    def finish(kind, slot, way, target):
        kv_copy(kind, slot, way, target).wait_send()

    def spread_out(kind, slot):
        for way in range(3):
            onward(kind, slot, way, start)

    def q_copy(slot, target):
        return remote(
            queries.at[pl.ds(slab_of(target), slab), :], q_rows.at[slot],
            q_send.at[target], q_recv.at[slot], "seq", target,
        )

    def head_at(index):
        return slice(index * head_size, (index + 1) * head_size)

    loads[2].wait()
    raw = dot(hidden[...], wqkv[1])
    for h in range(heads):
        kv[me, 0, :, head_at(h)] = scaled(raw[:, head_at(h)], k_gain_ref[...], 1.0)

    spread_out(0, me)

    loads[3].wait()
    kv[me, 1] = dot(hidden[...], wqkv[2]).astype(BF16)

    spread_out(1, me)

    loads[4].wait()
    raw = dot(hidden[...], wqkv[0])
    for h in range(heads):
        queries[:, head_at(h)] = scaled(
            raw[:, head_at(h)], q_gain_ref[...], 1.0 / math.sqrt(head_size)
        )
    q_rows[me] = queries[pl.ds(own_slab, slab), :]

    @pl.loop(1, n)
    def _(step):
        target = lax.rem(me + step, n)
        q_copy(me, target).start()

    oldest = head_ref[0]
    own_rank = lax.rem(me - oldest + n, n)

    for h in range(heads):
        weights = jnp.exp(dot_t(queries[:, head_at(h)], kv[me, 0, :, head_at(h)]))
        totals[:, head_at(h)] = weights
        acc[:, head_at(h)] = dot(weights.astype(BF16), kv[me, 1, :, head_at(h)])

    def absorb(source):
        rank = lax.rem(source - oldest + n, n)
        seen = jnp.full((rows, rows), rank, jnp.int32) <= own_rank
        for h in range(heads):
            scores = dot_t(queries[:, head_at(h)], kv[source, 0, :, head_at(h)])
            weights = jnp.where(seen, jnp.exp(scores), 0.0)
            totals[:, head_at(h)] += weights
            acc[:, head_at(h)] += dot(weights.astype(BF16), kv[source, 1, :, head_at(h)])

    def take_across(source):
        kv_copy(0, source, 2, me).wait_recv()
        kv_copy(1, source, 2, me).wait_recv()
        absorb(source)

    other = me + 1 - 2 * side

    @pl.loop(1, n // pair)
    def _(step):
        below, above = me - step * pair, me + step * pair
        for kind in range(2):

            @pl.when(below >= 0)
            def _():
                kv_copy(kind, below, 1, me).wait_recv()
                onward(kind, below, 1, start)
                onward(kind, below, 2, start)

            @pl.when(above < n)
            def _():
                kv_copy(kind, above, 0, me).wait_recv()
                onward(kind, above, 0, start)
                onward(kind, above, 2, start)

        @pl.when(step == 1)
        def _():
            take_across(other)

        @pl.when((step > 1) & (other - (step - 1) * pair >= 0))
        def _():
            take_across(other - (step - 1) * pair)

        @pl.when((step > 1) & (other + (step - 1) * pair < n))
        def _():
            take_across(other + (step - 1) * pair)

        @pl.when(below >= 0)
        def _():
            absorb(below)

        @pl.when(above < n)
        def _():
            absorb(above)

    last = n - pair

    @pl.when(other - last >= 0)
    def _():
        take_across(other - last)

    @pl.when(other + last < n)
    def _():
        take_across(other + last)

    @pl.loop(1, n)
    def _(step):
        source = lax.rem(me - step + n, n)
        q_copy(source, me).wait_recv()
        gate_copy(source, me).wait_recv()
        row_copy(source, me).wait_recv()

    for h in range(heads):
        total = jnp.sum(totals[:, head_at(h)], axis=-1, keepdims=True)
        attended[part, 0:rows, head_at(h)] = (acc[:, head_at(h)] / total).astype(BF16)
        weights = jnp.exp(dot_t(q_rows[oldest, :, head_at(h)], kv[oldest, 0, :, head_at(h)]))
        total = jnp.sum(weights, axis=-1, keepdims=True)
        product = dot(weights.astype(BF16), kv[oldest, 1, :, head_at(h)])
        attended[part, rows:, head_at(h)] = (product / total).astype(BF16)

    core = lax.rem(part, 2)
    sibling = part + 1 - 2 * core

    def att_copy(slot, target, way):
        return remote(
            attended.at[slot], attended.at[slot], att_send.at[way], att_recv.at[slot],
            "tensor", target,
        )

    ahead = [lax.rem(part + 2 * step, parts) for step in range(1, parts // 2)]
    for way, target in enumerate(ahead):
        att_copy(part, target, way).start()
    att_copy(part, sibling, len(ahead)).start()

    loads[5].wait()
    total = dot(attended[part], wout[part])

    def add(slot, total):
        w_copy(slot, part).wait_recv()
        return total + dot(attended[slot], wout[slot])

    att_copy(sibling, part, 0).wait_recv()
    total = add(sibling, total)
    for way, slot in enumerate(ahead):
        att_copy(slot, part, 0).wait_recv()
        att_copy(slot, sibling, len(ahead) + 1 + way).start()
        total = add(slot, total)
    for slot in ahead:
        handed = slot + 1 - 2 * core
        att_copy(handed, part, 0).wait_recv()
        total = add(handed, total)

    own_states = lat[:, pl.ds(first_column, columns)].astype(F32)
    updated = (own_states + gates[me] * total[0:rows]).astype(BF16)
    leaving = jnp.full((rows, columns), own_rank, jnp.int32) == 0
    loads[6].wait()
    updated_ref[0:rows, :] = jnp.where(leaving, noise[...], updated)
    updated_ref[rows:, :] = (
        lat_rows[oldest].astype(F32) + gates[oldest] * total[rows:]
    ).astype(BF16)

    for way in range(parts - 1):
        att_copy(part, sibling, way).wait_send()
    for step in range(1, parts):
        target = lax.rem(part + step, parts)
        mod_copy(part, target).wait_send()
        w_copy(part, target).wait_send()

    @pl.loop(1, n)
    def _(step):
        target = lax.rem(me + step, n)
        q_copy(me, target).wait_send()
        gate_copy(me, target).wait_send()
        row_copy(me, target).wait_send()

    for kind in range(2):
        for way in range(3):
            onward(kind, me, way, finish)

    @pl.loop(1, n // pair)
    def _(step):
        below, above = me - step * pair, me + step * pair
        for kind in range(2):

            @pl.when(below >= 0)
            def _():
                onward(kind, below, 1, finish)
                onward(kind, below, 2, finish)

            @pl.when(above < n)
            def _():
                onward(kind, above, 0, finish)
                onward(kind, above, 2, finish)


def finish_kernel(updated_ref, window_ref, clean_ref):
    rows = window_ref.shape[0]
    window_ref[...] = updated_ref[0:rows, :]
    clean_ref[...] = updated_ref[rows:, :]


def local(
    latents, levels, head_slot, fresh_noise, ada_weight, qkv_weight, q_gain, k_gain, out_weight
):
    n = lax.axis_size("seq")
    parts = lax.axis_size("tensor")
    rows, width = latents.shape
    columns = fresh_noise.shape[1]
    inner = out_weight.shape[0]
    clean_rows = rows // n
    slab = max(clean_rows, 16)
    vmem = pl.BlockSpec(memory_space=pltpu.VMEM)
    hbm = pl.BlockSpec(memory_space=pltpu.HBM)
    dma = pltpu.SemaphoreType.DMA
    updated = pl.pallas_call(
        functools.partial(kernel, n, parts, slab, clean_rows),
        out_shape=jax.ShapeDtypeStruct((rows + slab, columns), BF16),
        in_specs=[
            hbm, hbm, hbm, hbm, hbm, hbm, hbm, hbm, hbm,
        ],
        out_specs=vmem,
        scratch_shapes=[
            pltpu.SMEM((1,), jnp.int32),
            pltpu.SMEM((1,), jnp.int32),
            pltpu.VMEM((1, q_gain.shape[0]), F32),
            pltpu.VMEM((1, q_gain.shape[0]), F32),
            pltpu.VMEM((rows, columns), BF16),
            pltpu.VMEM((rows, width), BF16),
            pltpu.VMEM((3, ada_weight.shape[0], columns), BF16),
            pltpu.VMEM((3, width, inner), BF16),
            pltpu.VMEM((parts, inner, columns), BF16),
            pltpu.VMEM((rows, width), F32),
            pltpu.VMEM((rows, width), BF16),
            pltpu.VMEM((parts, 8, columns), F32),
            pltpu.VMEM((n, 1, columns), F32),
            pltpu.VMEM((n, slab, columns), BF16),
            pltpu.VMEM((n, 2, rows, inner), BF16),
            pltpu.VMEM((rows, inner), BF16),
            pltpu.VMEM((n, slab, inner), BF16),
            pltpu.VMEM((rows, inner), F32),
            pltpu.VMEM((rows, inner), F32),
            pltpu.VMEM((parts, rows + slab, inner), BF16),
            dma((11,)), dma((parts,)), dma((parts,)), dma((n,)), dma((n,)), dma((n,)), dma((n,)),
            dma((2, 3, n)), dma((2, n)), dma((n,)), dma((n,)), dma((parts,)), dma((parts,)),
            dma((parts,)), dma((parts,)),
        ],
        compiler_params=pltpu.CompilerParams(
            collective_id=0, has_side_effects=True, vmem_limit_bytes=60 * 1024 * 1024
        ),
    )(
        head_slot, levels, q_gain.reshape(1, -1), k_gain.reshape(1, -1), fresh_noise, latents,
        jnp.transpose(ada_weight, (1, 0, 2)), jnp.transpose(qkv_weight, (1, 0, 2)), out_weight,
    )
    window, clean = pl.pallas_call(
        finish_kernel,
        out_shape=(
            jax.ShapeDtypeStruct((rows, columns), BF16),
            jax.ShapeDtypeStruct((slab, columns), BF16),
        ),
        in_specs=[vmem],
        out_specs=(vmem, vmem),
    )(updated)
    if clean_rows < slab:
        start = (lax.axis_index("seq") * clean_rows) % slab
        clean = lax.dynamic_slice_in_dim(clean, start, clean_rows, 0)
    return window, clean


def solution(mesh):
    return jax.shard_map(
        local,
        mesh=mesh,
        in_specs=(
            P("seq", None),
            P("seq"),
            P(),
            P(None, "tensor"),
            P(None, None, "tensor"),
            P(None, None, "tensor"),
            P(),
            P(),
            P("tensor", None),
        ),
        out_specs=(P("seq", "tensor"), P("seq", "tensor")),
        check_vma=False,
    )
```

profile of v0, /device:TPU:1, one launch (start us, length us, event | category | flops | bytes accessed | tf_op | source)
XLA Modules:
  0.0 41.6 jit_solution(5494650961442272543)
XLA Ops:
  1.9 38.0 %shard_map.104.updated_ref = bf16[144,640]{1,0:T(8,128)(2,1)} custom-call(s32[1]{0:T(128)S(6)} %copy.12.head_hbm, s32[1]{0:T(128)S(6)} %copy.11.level_hbm, f32[1,128]{1,0:T(1,128)} %bitcast.6, f32[1,128]{1,0:T(1,128)} %bitcast.7, bf16[128,640]{1,0:T(8,128)(2,1)} %noise_hbm.1, bf16[128,2560]{1,0:T(8,128)(2,1)} %lat_hbm.1, bf16[3,256,640]{2,1,0:T(8,128)(2,1)} %bitcast.5, ...), custom_call_target="tpu_custom_call" | custom-call | tf_op jit(solution)/shard_map/pallas_call | solution.py:405
  40.0 1.6 %shard_map.105 = (bf16[128,640]{1,0:T(8,128)(2,1)}, bf16[16,640]{1,0:T(8,128)(2,1)}) custom-call(bf16[144,640]{1,0:T(8,128)(2,1)} %shard_map.104.updated_ref), custom_call_target="tpu_custom_call" | custom-call | tf_op jit(solution)/shard_map/pallas_call | solution.py:444
where the time goes:
time: 41.8 us; the launch traced here: 41.6 us
  Pallas kernels  39.7 us (95%)
  between operations  1.93 us (5%)
    pallas_call x1, Pallas kernels, local(): pl.pallas_call(functools.partial(kernel, n, parts, slab, clean_rows), out...  38 us
    pallas_call x1, Pallas kernels, local(): pl.pallas_call(finish_kernel, out_shape=(jax.ShapeDtypeStruct((rows, colu...  1.61 us

commit v1 on v0

v1 whole, which is shorter than its diff:
```python
import functools
import math

import jax
import jax.numpy as jnp
from jax import lax
from jax.experimental import pallas as pl
from jax.experimental.pallas import tpu as pltpu
from jax.sharding import PartitionSpec as P

F32 = jnp.float32
BF16 = jnp.bfloat16
EPS = 1e-06


def dot(a, b):
    return jnp.dot(a, b, preferred_element_type=F32)


def dot_t(a, b):
    return lax.dot_general(a, b, (((1,), (1,)), ((), ())), preferred_element_type=F32)


def kernel(
    n, parts, slab, clean_rows,
    head_hbm, level_hbm, q_gain_hbm, k_gain_hbm, noise_hbm, lat_hbm, ada_hbm, qkv_hbm, out_hbm,
    updated_ref,
    head_ref, level_ref, q_gain_ref, k_gain_ref, noise, lat, ada, wqkv, wout, normed, mods, gates,
    lat_rows, raw, stage, queries, kv, acc, totals, result, attended,
    load_sem, mod_send, mod_recv, gate_send, gate_recv, row_send, row_recv, w_send, w_recv,
    q_send, q_recv, kv_send, kv_recv, relay_send, back_send, att_recv, sib_send, cross_send,
):
    me = lax.axis_index("seq")
    part = lax.axis_index("tensor")
    pair = 2
    core = lax.rem(part, pair)
    plane = part // pair
    planes = parts // pair
    sibling = plane * pair + 1 - core
    rows, width = lat.shape
    columns = updated_ref.shape[1]
    head_size = q_gain_ref.shape[1]
    heads = stage.shape[1]
    half = rows // pair
    piece = half + slab
    owners = heads * pair
    first = (n - owners) // 2
    mine = me - first
    active = (mine >= 0) & (mine < owners)
    own_head = jnp.clip(mine // pair, 0, heads - 1)
    own_core = lax.rem(mine + owners * n, pair)

    def remote(src, dst, send, recv, target):
        return pltpu.make_async_remote_copy(
            src_ref=src, dst_ref=dst, send_sem=send, recv_sem=recv,
            device_id=target, device_id_type=pl.DeviceIdType.MESH,
        )

    def at_core(seq, which):
        return {"seq": seq, "tensor": plane * pair + which}

    loads = [
        pltpu.make_async_copy(ada_hbm, ada, load_sem.at[0]),
        pltpu.make_async_copy(lat_hbm, lat, load_sem.at[1]),
        pltpu.make_async_copy(qkv_hbm.at[0], wqkv.at[0], load_sem.at[2]),
        pltpu.make_async_copy(qkv_hbm.at[1], wqkv.at[1], load_sem.at[3]),
        pltpu.make_async_copy(qkv_hbm.at[2], wqkv.at[2], load_sem.at[4]),
        pltpu.make_async_copy(
            out_hbm.at[:, pl.ds(pl.multiple_of(part * columns, 128), columns)],
            wout.at[part], load_sem.at[5],
        ),
        pltpu.make_async_copy(noise_hbm, noise, load_sem.at[6]),
    ]
    small = [
        pltpu.make_async_copy(source, held, load_sem.at[7 + index])
        for index, (source, held) in enumerate((
            (level_hbm, level_ref), (head_hbm, head_ref),
            (q_gain_hbm, q_gain_ref), (k_gain_hbm, k_gain_ref),
        ))
    ]
    for load in small:
        load.start()
    for load in loads:
        load.start()

    barrier = pltpu.get_barrier_semaphore()
    for step in range(1, planes):
        for which in range(pair):
            pl.semaphore_signal(
                barrier, inc=1,
                device_id={"tensor": lax.rem(plane + step, planes) * pair + which},
                device_id_type=pl.DeviceIdType.MESH,
            )
    pl.semaphore_signal(
        barrier, inc=1, device_id={"tensor": sibling}, device_id_type=pl.DeviceIdType.MESH
    )

    @pl.loop(1, n)
    def _(step):
        for which in range(pair):
            pl.semaphore_signal(
                barrier, inc=1, device_id=at_core(lax.rem(me + step, n), which),
                device_id_type=pl.DeviceIdType.MESH,
            )

    for load in small:
        load.wait()
    half_width = ada.shape[1] // 2
    order = lax.broadcasted_iota(jnp.int32, (16, half_width), 1).astype(F32)
    angles = level_ref[0].astype(F32) * jnp.exp(-math.log(10000.0) * order / half_width)
    waves = jnp.concatenate([jnp.cos(angles), jnp.sin(angles)], axis=1)
    emb = (waves * (1.0 / (1.0 + jnp.exp(-waves)))).astype(BF16)
    loads[0].wait()
    for j in range(2):
        mods[part, j : j + 1, :] = dot(emb, ada[j])[0:1]
    gates[me] = dot(emb, ada[2])[0:1]

    pl.semaphore_wait(barrier, pair * n - 1 + parts - pair)

    def mod_copy(slot, target):
        return remote(
            mods.at[slot], mods.at[slot], mod_send.at[target], mod_recv.at[slot],
            {"tensor": target},
        )

    for step in range(1, parts):
        mod_copy(part, lax.rem(part + step, parts)).start()

    def slab_of(device):
        return pl.multiple_of((device * clean_rows) // slab * slab, slab)

    first_column = pl.multiple_of(part * columns, 128)

    def gate_copy(slot, target):
        return remote(
            gates.at[slot], gates.at[slot], gate_send.at[target], gate_recv.at[slot],
            {"seq": target},
        )

    def row_copy(slot, target):
        return remote(
            lat_hbm.at[pl.ds(slab_of(target), slab), pl.ds(first_column, columns)],
            lat_rows.at[slot], row_send.at[target], row_recv.at[slot], {"seq": target},
        )

    def w_copy(slot, target):
        at = pl.ds(pl.multiple_of(target * columns, 128), columns)
        return remote(
            out_hbm.at[:, at], wout.at[slot], w_send.at[target], w_recv.at[slot],
            {"tensor": target},
        )

    @pl.loop(1, n)
    def _(step):
        target = lax.rem(me + step, n)
        gate_copy(me, target).start()
        row_copy(me, target).start()

    for step in range(1, parts):
        w_copy(part, lax.rem(part + step, parts)).start()

    loads[1].wait()
    own_slab = slab_of(me)
    lat_rows[me] = lat[pl.ds(own_slab, slab), pl.ds(first_column, columns)]

    tile = 16

    @pl.loop(0, rows // tile, unroll=4)
    def _(index):
        at = pl.ds(pl.multiple_of(index * tile, tile), tile)
        states = lat[at, :].astype(F32)
        centered = states - jnp.mean(states, axis=-1, keepdims=True)
        variance = jnp.mean(centered * centered, axis=-1, keepdims=True)
        scaled_rows = centered * lax.rsqrt(variance + EPS)
        for index in range(parts):
            normed[index, at, :] = scaled_rows[:, index * columns : (index + 1) * columns]

    def hidden_of(slot):
        return (normed[slot] * (1.0 + mods[slot, 1:2, :]) + mods[slot, 0:1, :]).astype(BF16)

    own_hidden = hidden_of(part)
    for kind in range(3):
        loads[2 + kind].wait()
        raw[kind] = dot(own_hidden, wqkv[kind, part])
    mod_copy(sibling, part).wait_recv()
    sib_hidden = hidden_of(sibling)
    for kind in range(3):
        raw[kind] += dot(sib_hidden, wqkv[kind, sibling])

    others = [
        lax.rem(plane + step, planes) * pair + which
        for step in range(1, planes) for which in range(pair)
    ]
    for slot in others:
        mod_copy(slot, part).wait_recv()
    rest = [hidden_of(slot) for slot in others]

    def whole(kind):
        total = raw[kind]
        for hidden, slot in zip(rest, others):
            total = total + dot(hidden, wqkv[kind, slot])
        return total

    def scaled(matrix, gain, factor):
        power = jnp.mean(matrix * matrix, axis=-1, keepdims=True)
        return (matrix * lax.rsqrt(power + EPS) * gain * factor).astype(BF16)

    def head_at(index):
        return slice(index * head_size, (index + 1) * head_size)

    def turn(step):
        return jnp.where(me < n // 2, heads - 1 - step, step)

    def owner_of(h):
        return first + pair * h + core

    def q_copy(h, which, source):
        return remote(
            stage.at[0, h, pl.ds(pl.multiple_of(which * half, half), half)], queries.at[source],
            q_send.at[h, which], q_recv.at[source], at_core(owner_of(h), which),
        )

    def kv_copy(kind, h, source, which):
        return remote(
            stage.at[1 + kind, h], kv.at[kind, source], kv_send.at[kind, h],
            kv_recv.at[kind, source], at_core(owner_of(h), which),
        )

    def q_each(act):
        for step in range(heads):
            h = turn(step)
            for which in range(pair):

                @pl.when((owner_of(h) != me) | (core != which))
                def _():
                    act(q_copy(h, which, me))

    def kv_each(kind, act):
        for step in range(heads):
            h = turn(step)
            which = jnp.where(owner_of(h) == me, 1 - core, lax.rem(me, pair))
            act(kv_copy(kind, h, me, which))

    value = whole(0)
    for h in range(heads):
        stage[0, h] = scaled(value[:, head_at(h)], q_gain_ref[...], 1.0 / math.sqrt(head_size))
    q_each(lambda copy: copy.start())
    value = whole(1)
    for h in range(heads):
        stage[1, h] = scaled(value[:, head_at(h)], k_gain_ref[...], 1.0)
    kv_each(0, lambda copy: copy.start())
    value = whole(2)
    for h in range(heads):
        stage[2, h] = value[:, head_at(h)].astype(BF16)
    kv_each(1, lambda copy: copy.start())

    oldest = head_ref[0]

    def rank_of(block):
        return lax.rem(block - oldest + n, n)

    local_kv = active & (own_core == core)

    def relay(kind, source):
        return remote(
            kv.at[kind, source], kv.at[kind, source], relay_send.at[kind, source],
            kv_recv.at[kind, source], {"tensor": sibling},
        )

    def take(kind, source):
        @pl.when((source != me) | (own_core != core))
        def _():
            kv_copy(kind, 0, source, core).wait_recv()

    line = n // pair
    lane = lax.rem(me, pair)
    spot = me // pair

    def nearby(step, column):
        away = (step + 1) // 2 * (1 - 2 * lax.rem(step + 1, 2))
        return lax.rem(spot + away + n, line) * pair + column

    group = min(n, 8)

    def absorb(source):
        rank = rank_of(source)

        def some(base):
            at = pl.ds(base, group)
            q = queries[at].reshape(group * half, head_size)
            weights = jnp.exp(dot_t(q, kv[0, source])).reshape(group, half, head_size)
            weights = jnp.concatenate([
                jnp.where(
                    jnp.full((1, half, head_size), rank, jnp.int32) <= rank_of(base + index),
                    weights[index : index + 1], 0.0,
                )
                for index in range(group)
            ], axis=0)
            totals[at] += weights
            product = dot(
                weights.astype(BF16).reshape(group * half, head_size), kv[1, source]
            )
            acc[at] += product.reshape(group, half, head_size)

        if n == group:
            some(0)
        else:
            pl.loop(0, n // group)(lambda index: some(index * group))

    slot_at = plane * pair + own_core

    def back_copy(target):
        return remote(
            result.at[target],
            attended.at[slot_at, own_head, pl.ds(pl.multiple_of(core * piece, 16), piece)],
            back_send.at[target], att_recv.at[slot_at, own_head, core], at_core(target, core),
        )

    def far_order(step):
        return jnp.where(me < n // 2, n - 1 - step, step)


    @pl.when(active)
    def _():
        acc[...] = jnp.zeros_like(acc)
        totals[...] = jnp.zeros_like(totals)

        @pl.when(own_core == core)
        def _():
            queries[me] = stage[0, own_head, pl.ds(pl.multiple_of(core * half, half), half)]
            for kind in range(2):
                kv[kind, me] = stage[1 + kind, own_head]

        @pl.loop(0, n)
        def _(source):
            @pl.when((source != me) | (own_core != core))
            def _():
                q_copy(0, core, source).wait_recv()


        @pl.loop(0, line)
        def _(step):
            source = nearby(step, core)
            take(0, source)

            @pl.when(source != me)
            def _():
                relay(0, source).start()


        @pl.loop(0, line)
        def _(step):
            source = nearby(step, core)
            take(1, source)

            @pl.when(source != me)
            def _():
                relay(1, source).start()

            absorb(source)


        @pl.loop(0, line)
        def _(step):
            source = nearby(step, 1 - core)
            take(0, source)
            take(1, source)
            absorb(source)


        @pl.loop(0, n, unroll=min(n, 8))
        def _(block):
            total = jnp.sum(totals[block], axis=-1, keepdims=True)
            result[block, 0:half] = (acc[block] / total).astype(BF16)

        @pl.loop(0, n, unroll=min(n, 8))
        def _(block):
            at = pl.multiple_of(lax.rem(slab_of(block), half), slab)
            result[block, half:] = result[oldest, pl.ds(at, slab), :]

        @pl.loop(0, n)
        def _(step):
            target = far_order(step)

            @pl.when(target != me)
            def _():
                back_copy(target).start()

        attended[slot_at, own_head, pl.ds(pl.multiple_of(core * piece, 16), piece)] = result[me]

    for step in range(1, parts):
        target = lax.rem(part + step, parts)
        mod_copy(part, target).wait_send()
    q_each(lambda copy: copy.wait_send())
    kv_each(0, lambda copy: copy.wait_send())
    kv_each(1, lambda copy: copy.wait_send())

    @pl.loop(1, n)
    def _(step):
        target = lax.rem(me + step, n)
        source = lax.rem(me - step + n, n)
        gate_copy(me, target).wait_send()
        row_copy(me, target).wait_send()
        gate_copy(source, me).wait_recv()
        row_copy(source, me).wait_recv()

    def region(slot, h, which):
        return attended.at[slot, h, pl.ds(pl.multiple_of(which * piece, 16), piece)]

    def arrival(slot, h, which):
        held = region(slot, h, which)
        return remote(
            held, held, sib_send.at[slot, h], att_recv.at[slot, h, which], {"tensor": sibling}
        )

    def across(slot, h, step):
        held = region(slot, h, core)
        return remote(
            held, held, cross_send.at[step - 1, slot, h], att_recv.at[slot, h, core],
            {"tensor": lax.rem(plane + step, planes) * pair + core},
        )

    def ordered(step):
        g = jnp.where(me < n // 2, step, owners - 1 - step)
        return g, plane * pair + lax.rem(g, pair), g // pair

    for step in range(owners):
        g, slot, h = ordered(step)

        @pl.when(first + g != me)
        def _():
            arrival(slot, h, core).wait_recv()

        for way in range(1, planes):
            across(slot, h, way).start()
        arrival(slot, h, core).start()

    def slot_dot(slot):
        w_rows = wout[slot]
        joined = jnp.concatenate([attended[slot, h] for h in range(heads)], axis=1)
        return dot(joined, w_rows)

    for way in range(1, planes):
        for step in range(owners):
            g, slot, h = ordered(step)
            slot = lax.rem(slot + way * pair, parts)
            arrival(slot, h, core).wait_recv()
            arrival(slot, h, core).start()

    loads[5].wait()
    total = None
    for which in range(pair):
        slot = plane * pair + which
        for h in range(heads):
            arrival(slot, h, 1 - core).wait_recv()
    w_copy(sibling, part).wait_recv()
    total = slot_dot(part) + slot_dot(sibling)
    for slot in others:
        w_copy(slot, part).wait_recv()
    for slot in others:
        for h in range(heads):
            arrival(slot, h, 1 - core).wait_recv()
        total = total + slot_dot(slot)

    own_rank = rank_of(me)
    own_states = lat[:, pl.ds(first_column, columns)].astype(F32)
    mixed = jnp.concatenate([total[0:half], total[piece : piece + half]], axis=0)
    updated = (own_states + gates[me] * mixed).astype(BF16)
    leaving = jnp.full((rows, columns), own_rank, jnp.int32) == 0
    loads[6].wait()
    updated_ref[0:rows, :] = jnp.where(leaving, noise[...], updated)
    upper = jnp.full((slab, columns), own_slab, jnp.int32) >= half
    clean = jnp.where(upper, total[piece + half :], total[half:piece])
    updated_ref[rows:, :] = (
        lat_rows[oldest].astype(F32) + gates[oldest] * clean
    ).astype(BF16)

    for step in range(1, parts):
        w_copy(part, lax.rem(part + step, parts)).wait_send()
    for slot in range(parts):
        for h in range(heads):
            arrival(slot, h, core).wait_send()
    for way in range(1, planes):
        for step in range(owners):
            g, slot, h = ordered(step)
            across(slot, h, way).wait_send()

    @pl.when(active)
    def _():
        @pl.loop(0, n)
        def _(target):
            @pl.when(target != me)
            def _():
                back_copy(target).wait_send()

        @pl.loop(0, line)
        def _(step):
            source = nearby(step, core)

            @pl.when(source != me)
            def _():
                relay(0, source).wait_send()
                relay(1, source).wait_send()


def finish_kernel(updated_ref, window_ref, clean_ref):
    rows = window_ref.shape[0]
    window_ref[...] = updated_ref[0:rows, :]
    clean_ref[...] = updated_ref[rows:, :]


def local(
    latents, levels, head_slot, fresh_noise, ada_weight, qkv_weight, q_gain, k_gain, out_weight
):
    n = lax.axis_size("seq")
    parts = lax.axis_size("tensor")
    rows, width = latents.shape
    columns = fresh_noise.shape[1]
    inner = out_weight.shape[0]
    clean_rows = rows // n
    slab = max(clean_rows, 16)
    heads = inner // q_gain.shape[0]
    head_size = q_gain.shape[0]
    half = rows // 2
    vmem = pl.BlockSpec(memory_space=pltpu.VMEM)
    hbm = pl.BlockSpec(memory_space=pltpu.HBM)
    dma = pltpu.SemaphoreType.DMA
    updated = pl.pallas_call(
        functools.partial(kernel, n, parts, slab, clean_rows),
        out_shape=pltpu.VMEM((rows + slab, columns), BF16),
        in_specs=[
            hbm, hbm, hbm, hbm, hbm, hbm, hbm, hbm, hbm,
        ],
        out_specs=vmem,
        scratch_shapes=[
            pltpu.SMEM((1,), jnp.int32),
            pltpu.SMEM((1,), jnp.int32),
            pltpu.VMEM((1, head_size), F32),
            pltpu.VMEM((1, head_size), F32),
            pltpu.VMEM((rows, columns), BF16),
            pltpu.VMEM((rows, width), BF16),
            pltpu.VMEM((3, ada_weight.shape[0], columns), BF16),
            pltpu.VMEM((3, parts, columns, inner), BF16),
            pltpu.VMEM((parts, inner, columns), BF16),
            pltpu.VMEM((parts, rows, columns), F32),
            pltpu.VMEM((parts, 8, columns), F32),
            pltpu.VMEM((n, 1, columns), F32),
            pltpu.VMEM((n, slab, columns), BF16),
            pltpu.VMEM((3, rows, inner), F32),
            pltpu.VMEM((3, heads, rows, head_size), BF16),
            pltpu.VMEM((n, half, head_size), BF16),
            pltpu.VMEM((2, n, rows, head_size), BF16),
            pltpu.VMEM((n, half, head_size), F32),
            pltpu.VMEM((n, half, head_size), F32),
            pltpu.VMEM((n, half + slab, head_size), BF16),
            pltpu.VMEM((parts, heads, 2 * (half + slab), head_size), BF16),
            dma((11,)), dma((parts,)), dma((parts,)), dma((n,)), dma((n,)), dma((n,)), dma((n,)),
            dma((parts,)), dma((parts,)),
            dma((heads, 2)), dma((n,)), dma((2, heads)), dma((2, n)), dma((2, n)), dma((n,)),
            dma((parts, heads, 2)), dma((parts, heads)), dma((parts // 2 - 1, parts, heads)),
        ],
        compiler_params=pltpu.CompilerParams(
            collective_id=0, has_side_effects=True, vmem_limit_bytes=60 * 1024 * 1024
        ),
    )(
        head_slot, levels, q_gain.reshape(1, -1), k_gain.reshape(1, -1), fresh_noise, latents,
        jnp.transpose(ada_weight, (1, 0, 2)),
        jnp.transpose(qkv_weight, (1, 0, 2)).reshape(3, parts, columns, inner), out_weight,
    )
    updated = pltpu.with_memory_space_constraint(updated, pltpu.VMEM)
    window, clean = pl.pallas_call(
        finish_kernel,
        out_shape=(
            jax.ShapeDtypeStruct((rows, columns), BF16),
            jax.ShapeDtypeStruct((slab, columns), BF16),
        ),
        in_specs=[vmem],
        out_specs=(vmem, vmem),
    )(updated)
    if clean_rows < slab:
        start = (lax.axis_index("seq") * clean_rows) % slab
        clean = lax.dynamic_slice_in_dim(clean, start, clean_rows, 0)
    return window, clean


def solution(mesh):
    return jax.shard_map(
        local,
        mesh=mesh,
        in_specs=(
            P("seq", None),
            P("seq"),
            P(),
            P(None, "tensor"),
            P(None, None, "tensor"),
            P(None, None, "tensor"),
            P(),
            P(),
            P("tensor", None),
        ),
        out_specs=(P("seq", "tensor"), P("seq", "tensor")),
        check_vma=False,
    )
```

time: 41.8 us -> 38.6 us (0.923)
  Pallas kernels: 39.7 us -> 36.5 us
    pallas_call x1, Pallas kernels: 38 us -> 35.8 us  [local(): pl.pallas_call(functools.partial(kernel, n, parts, slab, clean_rows), out...]
    pallas_call x1, Pallas kernels: 1.61 us -> 0.68 us  [local(): pl.pallas_call(finish_kernel, out_shape=(jax.ShapeDtypeStruct((rows, colu...]
where the time goes in v1:
time: 38.6 us; the launch traced here: 38.4 us
  Pallas kernels  36.5 us (95%)
  between operations  1.93 us (5%)
    pallas_call x1, Pallas kernels, local(): pl.pallas_call(functools.partial(kernel, n, parts, slab, clean_rows), out...  35.8 us

profile of v1, /device:TPU:1, one launch (start us, length us, event | category | flops | bytes accessed | tf_op | source)
XLA Modules:
  0.0 38.4 jit_solution(10132164802390385339)
XLA Ops:
  1.9 35.8 %shard_map.104.updated_ref = bf16[144,640]{1,0:T(8,128)(2,1)S(1)} custom-call(s32[1]{0:T(128)S(6)} %copy.12.head_hbm, s32[1]{0:T(128)S(6)} %copy.11.level_hbm, f32[1,128]{1,0:T(1,128)} %bitcast.8, f32[1,128]{1,0:T(1,128)} %bitcast.9, bf16[128,640]{1,0:T(8,128)(2,1)} %noise_hbm.1, bf16[128,2560]{1,0:T(8,128)(2,1)} %lat_hbm.1, bf16[3,256,640]{2,1,0:T(8,128)(2,1)} %bitcast.7, ...), custom_call_target="tpu_custom_call" | custom-call | tf_op jit(solution)/shard_map/pallas_call | solution.py:528
  37.7 0.7 %shard_map.105 = (bf16[128,640]{1,0:T(8,128)(2,1)}, bf16[16,640]{1,0:T(8,128)(2,1)}) custom-call(bf16[144,640]{1,0:T(8,128)(2,1)S(1)} %shard_map.104.updated_ref), custom_call_target="tpu_custom_call" | custom-call | tf_op jit(solution)/shard_map/pallas_call | solution.py:571

commit v2 on v1

v2 whole, which is shorter than its diff:
```python
import functools
import math

import jax
import jax.numpy as jnp
from jax import lax
from jax.experimental import pallas as pl
from jax.experimental.pallas import tpu as pltpu
from jax.sharding import PartitionSpec as P

F32 = jnp.float32
BF16 = jnp.bfloat16
EPS = 1e-06


def dot(a, b):
    return jnp.dot(a, b, preferred_element_type=F32)


def dot_t(a, b):
    return lax.dot_general(a, b, (((1,), (1,)), ((), ())), preferred_element_type=F32)


def kernel(
    n, parts, slab, clean_rows,
    head_ref, level_ref, q_gain_hbm, k_gain_hbm, noise_hbm, lat_hbm, ada_hbm, qkv_hbm, out_hbm,
    updated_ref,
    gains, noise, lat, ada, wqkv, wout, normed, mods, gates,
    lat_rows, raw, stage, queries, kv, acc, totals, result, attended,
    load_sem, mod_send, mod_recv, gate_sem, row_sem, w_send, w_recv,
    q_sem, kv_send, kv_recv, relay_send, back_send, direct_recv, cross_recv, sib_recv, pass_send,
):
    me = lax.axis_index("seq")
    part = lax.axis_index("tensor")
    pair = 2
    core = lax.rem(part, pair)
    plane = part // pair
    planes = parts // pair
    sibling = plane * pair + 1 - core
    lane = lax.rem(me, pair)
    spot = me // pair
    line = n // pair
    buddy = me + 1 - pair * lane
    rows, width = lat.shape
    columns = updated_ref.shape[1]
    inner = wout.shape[1]
    head_size = gains.shape[2]
    heads = stage.shape[1]
    half = rows // pair
    piece = half + slab
    owners = heads * pair
    first = (n - owners) // 2
    mine = me - first
    active = (mine >= 0) & (mine < owners)
    own_head = jnp.clip(mine // pair, 0, heads - 1)
    own_core = lax.rem(mine + owners * n, pair)
    local = own_core == core
    others = [
        lax.rem(plane + step, planes) * pair + which
        for step in range(1, planes) for which in range(pair)
    ]

    def remote(src, dst, send, recv, target):
        return pltpu.make_async_remote_copy(
            src_ref=src, dst_ref=dst, send_sem=send, recv_sem=recv,
            device_id=target, device_id_type=pl.DeviceIdType.MESH,
        )

    def landed(ref, sem):
        remote(ref, ref, sem, sem, {"tensor": sibling}).wait_recv()

    def sent(ref, sem):
        remote(ref, ref, sem, sem, {"tensor": sibling}).wait_send()

    def at_core(seq, which):
        return {"seq": seq, "tensor": plane * pair + which}

    loads = [
        pltpu.make_async_copy(ada_hbm.at[0:2], ada.at[0:2], load_sem.at[0]),
        pltpu.make_async_copy(lat_hbm, lat, load_sem.at[1]),
        pltpu.make_async_copy(qkv_hbm.at[0], wqkv.at[0], load_sem.at[2]),
        pltpu.make_async_copy(qkv_hbm.at[1], wqkv.at[1], load_sem.at[3]),
        pltpu.make_async_copy(qkv_hbm.at[2], wqkv.at[2], load_sem.at[4]),
        pltpu.make_async_copy(ada_hbm.at[2], ada.at[2], load_sem.at[5]),
        pltpu.make_async_copy(q_gain_hbm, gains.at[0], load_sem.at[6]),
        pltpu.make_async_copy(k_gain_hbm, gains.at[1], load_sem.at[7]),
        pltpu.make_async_copy(
            out_hbm.at[:, pl.ds(pl.multiple_of(part * columns, 128), columns)],
            wout.at[part], load_sem.at[8],
        ),
        pltpu.make_async_copy(noise_hbm, noise, load_sem.at[9]),
    ]
    barrier = pltpu.get_barrier_semaphore()

    @pl.loop(1, n)
    def _(step):
        for which in range(pair):
            pl.semaphore_signal(
                barrier, inc=1, device_id=at_core(lax.rem(me + step, n), which),
                device_id_type=pl.DeviceIdType.MESH,
            )

    for slot in [sibling] + others:
        pl.semaphore_signal(
            barrier, inc=1, device_id={"tensor": slot}, device_id_type=pl.DeviceIdType.MESH
        )
    for load in loads:
        load.start()

    half_width = ada.shape[1] // 2
    order = lax.broadcasted_iota(jnp.int32, (16, half_width), 1).astype(F32)
    angles = level_ref[0].astype(F32) * jnp.exp(-math.log(10000.0) * order / half_width)
    waves = jnp.concatenate([jnp.cos(angles), jnp.sin(angles)], axis=1)
    emb = (waves * (1.0 / (1.0 + jnp.exp(-waves)))).astype(BF16)
    loads[0].wait()
    for j in range(2):
        mods[part, j : j + 1, :] = dot(emb, ada[j])[0:1]

    pl.semaphore_wait(barrier, pair * n - 1 + parts - pair)


    def mod_copy(target, near):
        return remote(
            mods.at[part], mods.at[part], mod_send.at[0], mod_recv.at[near], {"tensor": target}
        )

    for slot in others:
        mod_copy(slot, 1).start()
    mod_copy(sibling, 0).start()

    third = inner // 3 // 16 * 16
    own_third = pl.ds(pl.multiple_of(inner - (pair - lane) * third, 16), third)
    always = pl.ds(0, inner - pair * third)

    def w_copy(target, span, send, recv):
        at = pl.ds(pl.multiple_of(target * columns, 128), columns)
        return remote(
            out_hbm.at[span, at], wout.at[part, span], w_send.at[send], w_recv.at[recv],
            {"tensor": target},
        )

    for slot in others:
        w_copy(slot, own_third, 0, 0).start()
    for slot in others:
        w_copy(slot, always, 0, 1).start()
    w_copy(sibling, pl.ds(0, inner), 1, 2).start()

    def slab_of(device):
        return pl.multiple_of((device * clean_rows) // slab * slab, slab)

    first_column = pl.multiple_of(part * columns, 128)

    def row_copy(target):
        return remote(
            lat_hbm.at[pl.ds(slab_of(target), slab), pl.ds(first_column, columns)],
            lat_rows.at[me], row_sem.at[0], row_sem.at[1], {"seq": target},
        )

    def gate_copy(target):
        return remote(
            gates.at[me], gates.at[me], gate_sem.at[0], gate_sem.at[1], {"seq": target}
        )

    @pl.loop(1, n)
    def _(step):
        row_copy(lax.rem(me + step, n)).start()

    loads[1].wait()
    own_slab = slab_of(me)
    lat_rows[me] = lat[pl.ds(own_slab, slab), pl.ds(first_column, columns)]

    tile = 16

    @pl.loop(0, rows // tile, unroll=4)
    def _(index):
        at = pl.ds(pl.multiple_of(index * tile, tile), tile)
        states = lat[at, :].astype(F32)
        centered = states - jnp.mean(states, axis=-1, keepdims=True)
        variance = jnp.mean(centered * centered, axis=-1, keepdims=True)
        scaled_rows = centered * lax.rsqrt(variance + EPS)
        for index in range(parts):
            normed[index, at, :] = scaled_rows[:, index * columns : (index + 1) * columns]

    def hidden_of(slot):
        return (normed[slot] * (1.0 + mods[slot, 1:2, :]) + mods[slot, 0:1, :]).astype(BF16)

    own_hidden = hidden_of(part)
    for kind in range(3):
        loads[2 + kind].wait()
        raw[kind] = dot(own_hidden, wqkv[kind, part])
    loads[5].wait()
    gates[me] = dot(emb, ada[2])[0:1]

    @pl.loop(1, n)
    def _(step):
        gate_copy(lax.rem(me + step, n)).start()

    landed(mods.at[0], mod_recv.at[0])
    sib_hidden = hidden_of(sibling)
    for kind in range(3):
        raw[kind] += dot(sib_hidden, wqkv[kind, sibling])

    loads[6].wait()
    loads[7].wait()
    landed(mods.at[0 : parts - pair], mod_recv.at[1])
    rest = [hidden_of(slot) for slot in others]

    def whole(kind):
        total = raw[kind]
        for hidden, slot in zip(rest, others):
            total = total + dot(hidden, wqkv[kind, slot])
        return total

    def scaled(matrix, gain, factor):
        power = jnp.mean(matrix * matrix, axis=-1, keepdims=True)
        return (matrix * lax.rsqrt(power + EPS) * gain * factor).astype(BF16)

    def head_at(index):
        return slice(index * head_size, (index + 1) * head_size)

    def turn(step):
        return jnp.where(me < n // 2, heads - 1 - step, step)

    def owner_of(h):
        return first + pair * h + core

    def q_each(act):
        for step in range(heads):
            h = turn(step)
            for which in range(pair):

                @pl.when((owner_of(h) != me) | (core != which))
                def _():
                    act(remote(
                        stage.at[0, h, pl.ds(which * half, half)], queries.at[me],
                        q_sem.at[0], q_sem.at[1], at_core(owner_of(h), which),
                    ))

    def kv_each(kind, act):
        for step in range(heads):
            h = turn(step)
            owner = owner_of(h)
            which = jnp.where(owner == me, 1 - core, lane)
            relayed = jnp.where(which == lane, 0, 1)
            place = lane * line + lax.rem(spot - owner // pair + line, line)
            act(remote(
                stage.at[1 + kind, h], kv.at[kind, place], kv_send.at[0],
                kv_recv.at[kind, relayed], at_core(owner, which),
            ))

    value = whole(0)
    for h in range(heads):
        stage[0, h] = scaled(value[:, head_at(h)], gains[0], 1.0 / math.sqrt(head_size))
    q_each(lambda copy: copy.start())
    value = whole(1)
    for h in range(heads):
        stage[1, h] = scaled(value[:, head_at(h)], gains[1], 1.0)
    kv_each(0, lambda copy: copy.start())
    value = whole(2)
    for h in range(heads):
        stage[2, h] = value[:, head_at(h)].astype(BF16)
    kv_each(1, lambda copy: copy.start())

    landed(wout.at[0 : parts - pair, 0:third], w_recv.at[0])

    def w_pass(slot):
        held = wout.at[slot, own_third]
        return remote(held, held, w_send.at[2], w_recv.at[3], {"seq": buddy})

    for slot in others:
        w_pass(slot).start()

    oldest = head_ref[0]

    def rank_of(block):
        return lax.rem(block - oldest + n, n)

    def column_landed(kind, relayed, column):
        base = column * line

        @pl.when(local & (column == lane))
        def _():
            landed(kv.at[kind, 0 : line - 1], kv_recv.at[kind, relayed])

        @pl.when(jnp.logical_not(local & (column == lane)))
        def _():
            landed(kv.at[kind, 0:line], kv_recv.at[kind, relayed])

    def relay(kind, skip):
        held = kv.at[kind, pl.ds(core * line + skip, line - skip)]
        return remote(
            held, held, relay_send.at[0], kv_recv.at[kind, 1], {"tensor": sibling}
        )

    def relay_on(kind):
        @pl.when(core == lane)
        def _():
            relay(kind, 1).start()

        @pl.when(core != lane)
        def _():
            relay(kind, 0).start()

    slot_at = plane * pair + own_core
    own_piece = pl.ds(pl.multiple_of(core * piece, 16), piece)

    def back_copy(target):
        return remote(
            result.at[target], attended.at[slot_at, own_head, own_piece],
            back_send.at[0], direct_recv.at[own_head * pair + own_core], at_core(target, core),
        )

    span = min(line, 4)

    def absorb(column, base, count, fresh):
        def some(base, start, fresh):
            at = pl.ds(base, count)
            where = pl.ds(column * line + start, span)
            q = queries[at].reshape(count * half, head_size)
            scores = dot_t(q, kv[0, where].reshape(span * rows, head_size))
            ranks = [
                rank_of(lax.rem(spot + start + index, line) * pair + column)
                for index in range(span)
            ]
            joined = []
            for block in range(count):
                rank = rank_of(base + block)
                each = [
                    jnp.exp(
                        scores[block * half : (block + 1) * half, index * rows : (index + 1) * rows]
                        + jnp.where(ranks[index] <= rank, 0.0, -1e30)
                    )
                    for index in range(span)
                ]
                total = functools.reduce(jnp.add, each)
                totals[base + block] = total if fresh else totals[base + block] + total
                joined.append(jnp.concatenate([w.astype(BF16) for w in each], axis=1))
            product = dot(
                jnp.concatenate(joined, axis=0), kv[1, where].reshape(span * rows, head_size)
            ).reshape(count, half, head_size)
            acc[at] = product if fresh else acc[at] + product

        if line == span:
            some(base, 0, fresh)
        else:
            pl.loop(0, line // span)(lambda index: some(base, index * span, False))


    @pl.when(active)
    def _():
        if line != span:
            acc[...] = jnp.zeros_like(acc)
            totals[...] = jnp.zeros_like(totals)

        @pl.when(local)
        def _():
            queries[me] = stage[0, own_head, pl.ds(pl.multiple_of(core * half, half), half)]
            for kind in range(2):
                kv[kind, lane * line] = stage[1 + kind, own_head]
            landed(queries.at[0 : n - 1], q_sem.at[1])

        @pl.when(jnp.logical_not(local))
        def _():
            landed(queries, q_sem.at[1])

        column_landed(0, 0, core)
        relay_on(0)
        column_landed(1, 0, core)
        relay_on(1)
        blocks = min(n, 8)
        if n == blocks:
            absorb(core, 0, n, True)
        else:
            pl.loop(0, n // blocks)(lambda index: absorb(core, index * blocks, blocks, False))
        column_landed(0, 1, 1 - core)
        column_landed(1, 1, 1 - core)

        place = lax.rem(oldest, pair) * line + lax.rem(oldest // pair - spot + line, line)
        weights = jnp.exp(dot_t(queries[oldest], kv[0, place]))
        lead = dot(weights.astype(BF16), kv[1, place])
        lead = (lead / jnp.sum(weights, axis=-1, keepdims=True)).astype(BF16)

        def slab_fill(block):
            at = lax.rem(slab_of(block), half)
            chosen = lead[0:slab]
            for index in range(1, half // slab):
                chosen = jnp.where(
                    jnp.full((slab, head_size), at, jnp.int32) == index * slab,
                    lead[index * slab : (index + 1) * slab], chosen,
                )
            result[block, half:] = chosen

        batch = min(n // 2, 4)

        def batch_at(step):
            return jnp.where(me < n // 2, n // batch - 1 - step, step) * batch

        def last(step):
            base = batch_at(step)
            absorb(1 - core, base, batch, False)
            for index in range(batch):
                block = base + index
                total = jnp.sum(totals[block], axis=-1, keepdims=True)
                result[block, 0:half] = (acc[block] / total).astype(BF16)
                slab_fill(block)
            for index in range(batch):
                target = base + index

                @pl.when(target != me)
                def _():
                    back_copy(target).start()

        if n == 2 * batch:
            last(0)
            last(1)
        else:
            pl.loop(0, n // batch)(last)
        attended[slot_at, own_head, own_piece] = result[me]

    sent(mods.at[0 : parts - 1], mod_send.at[0])

    @pl.when(active & local)
    def _():
        sent(queries.at[0 : owners - 1], q_sem.at[0])

    @pl.when(jnp.logical_not(active & local))
    def _():
        sent(queries.at[0:owners], q_sem.at[0])

    sent(kv.at[:, 0:heads], kv_send.at[0])
    sent(gates.at[0 : n - 1], gate_sem.at[0])
    landed(gates.at[0 : n - 1], gate_sem.at[1])
    sent(lat_rows.at[0 : n - 1], row_sem.at[0])
    landed(lat_rows.at[0 : n - 1], row_sem.at[1])

    def region(slot, h):
        return attended.at[slot, h, own_piece]

    def to_sibling(slot, h, kind):
        held = region(slot, h)
        return remote(
            held, held, pass_send.at[0], sib_recv.at[kind], {"tensor": sibling}
        )

    def across(slot, h, g, step):
        held = region(slot, h)
        return remote(
            held, held, pass_send.at[1], cross_recv.at[step - 1, g],
            {"tensor": lax.rem(plane + step, planes) * pair + core},
        )

    def ordered(step):
        g = jnp.where(me < n // 2, step, owners - 1 - step)
        return g, plane * pair + lax.rem(g, pair), g // pair

    for step in range(owners):
        g, slot, h = ordered(step)

        @pl.when(first + g != me)
        def _():
            landed(region(slot, h), direct_recv.at[g])

        for way in range(1, planes):
            across(slot, h, g, way).start()
        to_sibling(slot, h, 0).start()

    def slot_dot(slot):
        joined = jnp.concatenate([attended[slot, h] for h in range(heads)], axis=1)
        return dot(joined, wout[slot])

    for way in range(1, planes):
        for step in range(owners):
            g, slot, h = ordered(step)
            slot = lax.rem(slot + (planes - way) * pair, parts)
            landed(region(slot, h), cross_recv.at[way - 1, g])
            to_sibling(slot, h, 1).start()

    loads[8].wait()
    landed(wout.at[0], w_recv.at[2])
    landed(attended.at[0:pair, :, 0:piece], sib_recv.at[0])
    total = slot_dot(part) + slot_dot(sibling)
    landed(wout.at[0 : parts - pair, always], w_recv.at[1])
    landed(wout.at[0 : parts - pair, 0:third], w_recv.at[3])
    landed(attended.at[0 : parts - pair, :, 0:piece], sib_recv.at[1])
    for slot in others:
        total = total + slot_dot(slot)

    own_rank = rank_of(me)
    own_states = lat[:, pl.ds(first_column, columns)].astype(F32)
    mixed = jnp.concatenate([total[0:half], total[piece : piece + half]], axis=0)
    updated = (own_states + gates[me] * mixed).astype(BF16)
    leaving = jnp.full((rows, columns), own_rank, jnp.int32) == 0
    loads[9].wait()
    updated_ref[0:rows, :] = jnp.where(leaving, noise[...], updated)
    upper = jnp.full((slab, columns), own_slab, jnp.int32) >= half
    clean = jnp.where(upper, total[piece + half :], total[half:piece])
    updated_ref[rows:, :] = (
        lat_rows[oldest].astype(F32) + gates[oldest] * clean
    ).astype(BF16)

    sent(wout.at[0 : parts - pair, 0 : inner - third], w_send.at[0])
    sent(wout.at[0], w_send.at[1])
    sent(wout.at[0 : parts - pair, 0:third], w_send.at[2])
    sent(attended.at[:, :, 0:piece], pass_send.at[0])
    sent(attended.at[0 : parts - pair, :, 0:piece], pass_send.at[1])

    @pl.when(active)
    def _():
        sent(result.at[0 : n - 1], back_send.at[0])

        @pl.when(core == lane)
        def _():
            sent(kv.at[:, 0 : line - 1], relay_send.at[0])

        @pl.when(core != lane)
        def _():
            sent(kv.at[:, 0:line], relay_send.at[0])


def finish_kernel(updated_ref, window_ref, clean_ref):
    rows = window_ref.shape[0]
    window_ref[...] = updated_ref[0:rows, :]
    clean_ref[...] = updated_ref[rows:, :]


def local(
    latents, levels, head_slot, fresh_noise, ada_weight, qkv_weight, q_gain, k_gain, out_weight
):
    n = lax.axis_size("seq")
    parts = lax.axis_size("tensor")
    rows, width = latents.shape
    columns = fresh_noise.shape[1]
    inner = out_weight.shape[0]
    clean_rows = rows // n
    slab = max(clean_rows, 16)
    heads = inner // q_gain.shape[0]
    head_size = q_gain.shape[0]
    half = rows // 2
    owners = 2 * heads
    vmem = pl.BlockSpec(memory_space=pltpu.VMEM)
    smem = pl.BlockSpec(memory_space=pltpu.SMEM)
    hbm = pl.BlockSpec(memory_space=pltpu.HBM)
    dma = pltpu.SemaphoreType.DMA
    updated = pl.pallas_call(
        functools.partial(kernel, n, parts, slab, clean_rows),
        out_shape=pltpu.VMEM((rows + slab, columns), BF16),
        in_specs=[
            smem, smem, hbm, hbm, hbm, hbm, hbm, hbm, hbm,
        ],
        out_specs=vmem,
        scratch_shapes=[
            pltpu.VMEM((2, 1, head_size), F32),
            pltpu.VMEM((rows, columns), BF16),
            pltpu.VMEM((rows, width), BF16),
            pltpu.VMEM((3, ada_weight.shape[0], columns), BF16),
            pltpu.VMEM((3, parts, columns, inner), BF16),
            pltpu.VMEM((parts, inner, columns), BF16),
            pltpu.VMEM((parts, rows, columns), F32),
            pltpu.VMEM((parts, 2, columns), F32),
            pltpu.VMEM((n, 1, columns), F32),
            pltpu.VMEM((n, slab, columns), BF16),
            pltpu.VMEM((3, rows, inner), F32),
            pltpu.VMEM((3, heads, rows, head_size), BF16),
            pltpu.VMEM((n, half, head_size), BF16),
            pltpu.VMEM((2, n, rows, head_size), BF16),
            pltpu.VMEM((n, half, head_size), F32),
            pltpu.VMEM((n, half, rows), F32),
            pltpu.VMEM((n, half + slab, head_size), BF16),
            pltpu.VMEM((parts, heads, 2 * (half + slab), head_size), BF16),
            dma((10,)), dma((1,)), dma((2,)), dma((2,)), dma((2,)), dma((3,)), dma((4,)),
            dma((2,)), dma((1,)), dma((2, 2)), dma((1,)), dma((1,)), dma((owners,)),
            dma((parts // 2 - 1, owners)), dma((2,)), dma((2,)),
        ],
        compiler_params=pltpu.CompilerParams(
            collective_id=0, has_side_effects=True, vmem_limit_bytes=60 * 1024 * 1024
        ),
    )(
        head_slot, levels, q_gain.reshape(1, -1), k_gain.reshape(1, -1), fresh_noise, latents,
        jnp.transpose(ada_weight, (1, 0, 2)),
        jnp.transpose(qkv_weight, (1, 0, 2)).reshape(3, parts, columns, inner), out_weight,
    )
    updated = pltpu.with_memory_space_constraint(updated, pltpu.VMEM)
    window, clean = pl.pallas_call(
        finish_kernel,
        out_shape=(
            jax.ShapeDtypeStruct((rows, columns), BF16),
            jax.ShapeDtypeStruct((slab, columns), BF16),
        ),
        in_specs=[vmem],
        out_specs=(vmem, vmem),
    )(updated)
    if clean_rows < slab:
        start = (lax.axis_index("seq") * clean_rows) % slab
        clean = lax.dynamic_slice_in_dim(clean, start, clean_rows, 0)
    return window, clean


def solution(mesh):
    return jax.shard_map(
        local,
        mesh=mesh,
        in_specs=(
            P("seq", None),
            P("seq"),
            P(),
            P(None, "tensor"),
            P(None, None, "tensor"),
            P(None, None, "tensor"),
            P(),
            P(),
            P("tensor", None),
        ),
        out_specs=(P("seq", "tensor"), P("seq", "tensor")),
        check_vma=False,
    )
```

time: 38.6 us -> 32.8 us (0.85)
  Pallas kernels: 36.5 us -> 30.7 us
    pallas_call x1, Pallas kernels: 35.8 us -> 30.1 us  [local(): pl.pallas_call(functools.partial(kernel, n, parts, slab, clean_rows), out...]
where the time goes in v2:
time: 32.8 us; the launch traced here: 32.7 us
  Pallas kernels  30.7 us (94%)
  between operations  1.93 us (6%)
    pallas_call x1, Pallas kernels, local(): pl.pallas_call(functools.partial(kernel, n, parts, slab, clean_rows), out...  30.1 us
    pallas_call x1, Pallas kernels, local(): pl.pallas_call(finish_kernel, out_shape=(jax.ShapeDtypeStruct((rows, colu...  0.68 us

profile of v2, /device:TPU:1, one launch (start us, length us, event | category | flops | bytes accessed | tf_op | source)
XLA Modules:
  0.0 32.7 jit_solution(2223163443734987170)
XLA Ops:
  1.9 30.1 %shard_map.104.updated_ref = bf16[144,640]{1,0:T(8,128)(2,1)S(1)} custom-call(s32[1]{0:T(128)S(6)} %copy.12.head_ref, s32[1]{0:T(128)S(6)} %copy.11.level_ref, f32[1,128]{1,0:T(1,128)} %bitcast.8, f32[1,128]{1,0:T(1,128)} %bitcast.9, bf16[128,640]{1,0:T(8,128)(2,1)} %noise_hbm.1, bf16[128,2560]{1,0:T(8,128)(2,1)} %lat_hbm.1, bf16[3,256,640]{2,1,0:T(8,128)(2,1)} %bitcast.7, ...), custom_call_target="tpu_custom_call" | custom-call | tf_op jit(solution)/shard_map/pallas_call | solution.py:544
  32.0 0.7 %shard_map.105 = (bf16[128,640]{1,0:T(8,128)(2,1)}, bf16[16,640]{1,0:T(8,128)(2,1)}) custom-call(bf16[144,640]{1,0:T(8,128)(2,1)S(1)} %shard_map.104.updated_ref), custom_call_target="tpu_custom_call" | custom-call | tf_op jit(solution)/shard_map/pallas_call | solution.py:583

commit v3 on v2

--- a/solution.py
+++ b/solution.py
@@ -26,8 +26,8 @@
     head_ref, level_ref, q_gain_hbm, k_gain_hbm, noise_hbm, lat_hbm, ada_hbm, qkv_hbm, out_hbm,
     updated_ref,
     gains, noise, lat, ada, wqkv, wout, normed, mods, gates,
-    lat_rows, raw, stage, queries, kv, acc, totals, result, attended,
-    load_sem, mod_send, mod_recv, gate_sem, row_sem, w_send, w_recv,
+    lat_rows, mixed_rows, clean_rows_ref, raw, stage, queries, kv, acc, totals, result, attended,
+    ready, load_sem, mod_send, mod_recv, gate_sem, row_sem, w_send, w_recv,
     q_sem, kv_send, kv_recv, relay_send, back_send, direct_recv, cross_recv, sib_recv, pass_send,
 ):
     me = lax.axis_index("seq")
@@ -56,7 +56,7 @@
     own_core = lax.rem(mine + owners * n, pair)
     local = own_core == core
     others = [
-        lax.rem(plane + step, planes) * pair + which
+        lax.rem(plane + step, planes) * pair + lax.rem(core + which, pair)
         for step in range(1, planes) for which in range(pair)
     ]
 
@@ -94,16 +94,20 @@
 
     @pl.loop(1, n)
     def _(step):
-        for which in range(pair):
+        pl.semaphore_signal(
+            barrier, inc=1, device_id=at_core(lax.rem(me + step, n), pair - 1),
+            device_id_type=pl.DeviceIdType.MESH,
+        )
+
+    for step in range(planes):
+        slot = lax.rem(plane + step, planes) * pair
+
+        @pl.when(slot != part)
+        def _():
             pl.semaphore_signal(
-                barrier, inc=1, device_id=at_core(lax.rem(me + step, n), which),
-                device_id_type=pl.DeviceIdType.MESH,
+                barrier, inc=1, device_id={"tensor": slot}, device_id_type=pl.DeviceIdType.MESH
             )
 
-    for slot in [sibling] + others:
-        pl.semaphore_signal(
-            barrier, inc=1, device_id={"tensor": slot}, device_id_type=pl.DeviceIdType.MESH
-        )
     for load in loads:
         load.start()
 
@@ -116,7 +120,29 @@
     for j in range(2):
         mods[part, j : j + 1, :] = dot(emb, ada[j])[0:1]
 
-    pl.semaphore_wait(barrier, pair * n - 1 + parts - pair)
+    def tell_sibling():
+        pl.semaphore_signal(
+            ready, inc=1, device_id={"tensor": sibling}, device_id_type=pl.DeviceIdType.MESH
+        )
+
+    @pl.when(core == 0)
+    def _():
+        pl.semaphore_wait(barrier, parts - 1)
+        tell_sibling()
+
+    @pl.when(core != 0)
+    def _():
+        pl.semaphore_wait(ready, 1)
+
+    def meet():
+        @pl.when(core != 0)
+        def _():
+            pl.semaphore_wait(barrier, pair * (n - 1))
+            tell_sibling()
+
+        @pl.when(core == 0)
+        def _():
+            pl.semaphore_wait(ready, 1)
 
 
     def mod_copy(target, near):
@@ -139,8 +165,8 @@
             {"tensor": target},
         )
 
-    for slot in others:
-        w_copy(slot, own_third, 0, 0).start()
+    for index, slot in enumerate(others):
+        w_copy(slot, own_third, 0, 4 + index).start()
     for slot in others:
         w_copy(slot, always, 0, 1).start()
     w_copy(sibling, pl.ds(0, inner), 1, 2).start()
@@ -150,24 +176,19 @@
 
     first_column = pl.multiple_of(part * columns, 128)
 
-    def row_copy(target):
-        return remote(
-            lat_hbm.at[pl.ds(slab_of(target), slab), pl.ds(first_column, columns)],
-            lat_rows.at[me], row_sem.at[0], row_sem.at[1], {"seq": target},
+    def swap_copy(step):
+        return remote(
+            lat_hbm.at[pl.ds(slab_of(step * pair + 1 - lane), slab), pl.ds(first_column, columns)],
+            lat_rows.at[step], row_sem.at[0], row_sem.at[1], {"seq": buddy},
         )
 
     def gate_copy(target):
         return remote(
             gates.at[me], gates.at[me], gate_sem.at[0], gate_sem.at[1], {"seq": target}
         )
-
-    @pl.loop(1, n)
-    def _(step):
-        row_copy(lax.rem(me + step, n)).start()
 
     loads[1].wait()
     own_slab = slab_of(me)
-    lat_rows[me] = lat[pl.ds(own_slab, slab), pl.ds(first_column, columns)]
 
     tile = 16
 
@@ -188,13 +209,6 @@
     for kind in range(3):
         loads[2 + kind].wait()
         raw[kind] = dot(own_hidden, wqkv[kind, part])
-    loads[5].wait()
-    gates[me] = dot(emb, ada[2])[0:1]
-
-    @pl.loop(1, n)
-    def _(step):
-        gate_copy(lax.rem(me + step, n)).start()
-
     landed(mods.at[0], mod_recv.at[0])
     sib_hidden = hidden_of(sibling)
     for kind in range(3):
@@ -251,6 +265,7 @@
     value = whole(0)
     for h in range(heads):
         stage[0, h] = scaled(value[:, head_at(h)], gains[0], 1.0 / math.sqrt(head_size))
+    meet()
     q_each(lambda copy: copy.start())
     value = whole(1)
     for h in range(heads):
@@ -261,16 +276,15 @@
         stage[2, h] = value[:, head_at(h)].astype(BF16)
     kv_each(1, lambda copy: copy.start())
 
-    landed(wout.at[0 : parts - pair, 0:third], w_recv.at[0])
-
-    def w_pass(slot):
+    @pl.loop(0, line)
+    def _(step):
+        swap_copy(step).start()
+
+    oldest = head_ref[0]
+    for index, slot in enumerate(others):
         held = wout.at[slot, own_third]
-        return remote(held, held, w_send.at[2], w_recv.at[3], {"seq": buddy})
-
-    for slot in others:
-        w_pass(slot).start()
-
-    oldest = head_ref[0]
+        landed(held, w_recv.at[4 + index])
+        remote(held, held, w_send.at[2], w_recv.at[3], {"seq": buddy}).start()
 
     def rank_of(block):
         return lax.rem(block - oldest + n, n)
@@ -417,21 +431,30 @@
             pl.loop(0, n // batch)(last)
         attended[slot_at, own_head, own_piece] = result[me]
 
-    sent(mods.at[0 : parts - 1], mod_send.at[0])
-
-    @pl.when(active & local)
-    def _():
-        sent(queries.at[0 : owners - 1], q_sem.at[0])
-
-    @pl.when(jnp.logical_not(active & local))
-    def _():
-        sent(queries.at[0:owners], q_sem.at[0])
-
-    sent(kv.at[:, 0:heads], kv_send.at[0])
-    sent(gates.at[0 : n - 1], gate_sem.at[0])
-    landed(gates.at[0 : n - 1], gate_sem.at[1])
-    sent(lat_rows.at[0 : n - 1], row_sem.at[0])
-    landed(lat_rows.at[0 : n - 1], row_sem.at[1])
+    landed(lat_rows, row_sem.at[1])
+    swapped = jnp.full((slab, columns), buddy, jnp.int32) == oldest
+    for step in range(line):
+        target = step * pair + lane
+        kept = lat[pl.ds(slab_of(target), slab), pl.ds(first_column, columns)]
+        mixed_rows[step] = jnp.where(swapped, lat_rows[step], kept)
+    clean_rows_ref[spot] = mixed_rows[spot]
+
+    def row_copy(target_spot):
+        return remote(
+            mixed_rows.at[target_spot], clean_rows_ref.at[spot], row_sem.at[2], row_sem.at[3],
+            {"seq": target_spot * pair + lane},
+        )
+
+    @pl.loop(1, line)
+    def _(step):
+        row_copy(lax.rem(spot + step, line)).start()
+
+    loads[5].wait()
+    gates[me] = dot(emb, ada[2])[0:1]
+
+    @pl.loop(1, n)
+    def _(step):
+        gate_copy(lax.rem(me + step, n)).start()
 
     def region(slot, h):
         return attended.at[slot, h, own_piece]
@@ -450,7 +473,7 @@
         )
 
     def ordered(step):
-        g = jnp.where(me < n // 2, step, owners - 1 - step)
+        g = jnp.where(me < n // 2, owners - 1 - step, step)
         return g, plane * pair + lax.rem(g, pair), g // pair
 
     for step in range(owners):
@@ -485,19 +508,35 @@
     for slot in others:
         total = total + slot_dot(slot)
 
+    landed(gates.at[0 : n - 1], gate_sem.at[1])
+    landed(lat_rows.at[0 : line - 1], row_sem.at[3])
+    loads[9].wait()
     own_rank = rank_of(me)
     own_states = lat[:, pl.ds(first_column, columns)].astype(F32)
     mixed = jnp.concatenate([total[0:half], total[piece : piece + half]], axis=0)
     updated = (own_states + gates[me] * mixed).astype(BF16)
     leaving = jnp.full((rows, columns), own_rank, jnp.int32) == 0
-    loads[9].wait()
     updated_ref[0:rows, :] = jnp.where(leaving, noise[...], updated)
     upper = jnp.full((slab, columns), own_slab, jnp.int32) >= half
     clean = jnp.where(upper, total[piece + half :], total[half:piece])
     updated_ref[rows:, :] = (
-        lat_rows[oldest].astype(F32) + gates[oldest] * clean
+        clean_rows_ref[oldest // pair].astype(F32) + gates[oldest] * clean
     ).astype(BF16)
 
+    sent(mods.at[0 : parts - 1], mod_send.at[0])
+
+    @pl.when(active & local)
+    def _():
+        sent(queries.at[0 : owners - 1], q_sem.at[0])
+
+    @pl.when(jnp.logical_not(active & local))
+    def _():
+        sent(queries.at[0:owners], q_sem.at[0])
+
+    sent(kv.at[:, 0:heads], kv_send.at[0])
+    sent(gates.at[0 : n - 1], gate_sem.at[0])
+    sent(lat_rows, row_sem.at[0])
+    sent(lat_rows.at[0 : line - 1], row_sem.at[2])
     sent(wout.at[0 : parts - pair, 0 : inner - third], w_send.at[0])
     sent(wout.at[0], w_send.at[1])
     sent(wout.at[0 : parts - pair, 0:third], w_send.at[2])
@@ -558,7 +597,9 @@
             pltpu.VMEM((parts, rows, columns), F32),
             pltpu.VMEM((parts, 2, columns), F32),
             pltpu.VMEM((n, 1, columns), F32),
-            pltpu.VMEM((n, slab, columns), BF16),
+            pltpu.VMEM((n // 2, slab, columns), BF16),
+            pltpu.VMEM((n // 2, slab, columns), BF16),
+            pltpu.VMEM((n // 2, slab, columns), BF16),
             pltpu.VMEM((3, rows, inner), F32),
             pltpu.VMEM((3, heads, rows, head_size), BF16),
             pltpu.VMEM((n, half, head_size), BF16),
@@ -567,7 +608,7 @@
             pltpu.VMEM((n, half, rows), F32),
             pltpu.VMEM((n, half + slab, head_size), BF16),
             pltpu.VMEM((parts, heads, 2 * (half + slab), head_size), BF16),
-            dma((10,)), dma((1,)), dma((2,)), dma((2,)), dma((2,)), dma((3,)), dma((4,)),
+            pltpu.SemaphoreType.REGULAR, dma((10,)), dma((1,)), dma((2,)), dma((2,)), dma((4,)), dma((3,)), dma((4 + parts - 2,)),
             dma((2,)), dma((1,)), dma((2, 2)), dma((1,)), dma((1,)), dma((owners,)),
             dma((parts // 2 - 1, owners)), dma((2,)), dma((2,)),
         ],

time: 32.8 us -> 30.6 us (0.933)
  Pallas kernels: 30.7 us -> 28.4 us
    pallas_call x1, Pallas kernels: 30.1 us -> 27.8 us  [local(): pl.pallas_call(functools.partial(kernel, n, parts, slab, clean_rows), out...]
where the time goes in v3:
time: 30.6 us; the launch traced here: 30.4 us
  Pallas kernels  28.4 us (93%)
  between operations  1.93 us (6%)
    pallas_call x1, Pallas kernels, local(): pl.pallas_call(functools.partial(kernel, n, parts, slab, clean_rows), out...  27.8 us
    pallas_call x1, Pallas kernels, local(): pl.pallas_call(finish_kernel, out_shape=(jax.ShapeDtypeStruct((rows, colu...  0.68 us

profile of v3, /device:TPU:1, one launch (start us, length us, event | category | flops | bytes accessed | tf_op | source)
XLA Modules:
  0.0 30.4 jit_solution(12328282823426378021)
XLA Ops:
  1.9 27.8 %shard_map.104.updated_ref = bf16[144,640]{1,0:T(8,128)(2,1)S(1)} custom-call(s32[1]{0:T(128)S(6)} %copy.12.head_ref, s32[1]{0:T(128)S(6)} %copy.11.level_ref, f32[1,128]{1,0:T(1,128)} %bitcast.8, f32[1,128]{1,0:T(1,128)} %bitcast.9, bf16[128,640]{1,0:T(8,128)(2,1)} %noise_hbm.1, bf16[128,2560]{1,0:T(8,128)(2,1)} %lat_hbm.1, bf16[3,256,640]{2,1,0:T(8,128)(2,1)} %bitcast.7, ...), custom_call_target="tpu_custom_call" | custom-call | tf_op jit(solution)/shard_map/pallas_call | solution.py:583
  29.7 0.7 %shard_map.105 = (bf16[128,640]{1,0:T(8,128)(2,1)}, bf16[16,640]{1,0:T(8,128)(2,1)}) custom-call(bf16[144,640]{1,0:T(8,128)(2,1)S(1)} %shard_map.104.updated_ref), custom_call_target="tpu_custom_call" | custom-call | tf_op jit(solution)/shard_map/pallas_call | solution.py:624

commit v4 on v3

--- a/solution.py
+++ b/solution.py
@@ -26,10 +26,11 @@
     head_ref, level_ref, q_gain_hbm, k_gain_hbm, noise_hbm, lat_hbm, ada_hbm, qkv_hbm, out_hbm,
     updated_ref,
     gains, noise, lat, ada, wqkv, wout, normed, mods, gates,
-    lat_rows, mixed_rows, clean_rows_ref, raw, stage, queries, kv, acc, totals, result, attended,
+    lat_rows, mixed_rows, clean_rows_ref, raw, stage, queries, keys, values, acc, totals, seen, result, attended, partial,
     ready, load_sem, mod_send, mod_recv, gate_sem, row_sem, w_send, w_recv,
     q_sem, kv_send, kv_recv, relay_send, back_send, direct_recv, cross_recv, sib_recv, pass_send,
 ):
+    kv = (keys, values)
     me = lax.axis_index("seq")
     part = lax.axis_index("tensor")
     pair = 2
@@ -92,6 +93,19 @@
     ]
     barrier = pltpu.get_barrier_semaphore()
 
+    loads[0].start()
+    for step in range(planes):
+        slot = lax.rem(plane + step, planes) * pair
+
+        @pl.when(slot != part)
+        def _():
+            pl.semaphore_signal(
+                barrier, inc=1, device_id={"tensor": slot}, device_id_type=pl.DeviceIdType.MESH
+            )
+
+    for load in loads[1:5]:
+        load.start()
+
     @pl.loop(1, n)
     def _(step):
         pl.semaphore_signal(
@@ -99,27 +113,12 @@
             device_id_type=pl.DeviceIdType.MESH,
         )
 
-    for step in range(planes):
-        slot = lax.rem(plane + step, planes) * pair
-
-        @pl.when(slot != part)
-        def _():
-            pl.semaphore_signal(
-                barrier, inc=1, device_id={"tensor": slot}, device_id_type=pl.DeviceIdType.MESH
-            )
-
-    for load in loads:
-        load.start()
 
     half_width = ada.shape[1] // 2
     order = lax.broadcasted_iota(jnp.int32, (16, half_width), 1).astype(F32)
     angles = level_ref[0].astype(F32) * jnp.exp(-math.log(10000.0) * order / half_width)
     waves = jnp.concatenate([jnp.cos(angles), jnp.sin(angles)], axis=1)
     emb = (waves * (1.0 / (1.0 + jnp.exp(-waves)))).astype(BF16)
-    loads[0].wait()
-    for j in range(2):
-        mods[part, j : j + 1, :] = dot(emb, ada[j])[0:1]
-
     def tell_sibling():
         pl.semaphore_signal(
             ready, inc=1, device_id={"tensor": sibling}, device_id_type=pl.DeviceIdType.MESH
@@ -133,6 +132,10 @@
     @pl.when(core != 0)
     def _():
         pl.semaphore_wait(ready, 1)
+
+    loads[0].wait()
+    for j in range(2):
+        mods[part, j : j + 1, :] = dot(emb, ada[j])[0:1]
 
     def meet():
         @pl.when(core != 0)
@@ -169,7 +172,6 @@
         w_copy(slot, own_third, 0, 4 + index).start()
     for slot in others:
         w_copy(slot, always, 0, 1).start()
-    w_copy(sibling, pl.ds(0, inner), 1, 2).start()
 
     def slab_of(device):
         return pl.multiple_of((device * clean_rows) // slab * slab, slab)
@@ -209,6 +211,8 @@
     for kind in range(3):
         loads[2 + kind].wait()
         raw[kind] = dot(own_hidden, wqkv[kind, part])
+    for load in loads[5:]:
+        load.start()
     landed(mods.at[0], mod_recv.at[0])
     sib_hidden = hidden_of(sibling)
     for kind in range(3):
@@ -238,49 +242,59 @@
     def owner_of(h):
         return first + pair * h + core
 
-    def q_each(act):
-        for step in range(heads):
-            h = turn(step)
+    def send(kind, step):
+        h = turn(step)
+        owner = owner_of(h)
+        if kind == 0:
             for which in range(pair):
 
-                @pl.when((owner_of(h) != me) | (core != which))
+                @pl.when((owner != me) | (core != which))
                 def _():
-                    act(remote(
+                    remote(
                         stage.at[0, h, pl.ds(which * half, half)], queries.at[me],
-                        q_sem.at[0], q_sem.at[1], at_core(owner_of(h), which),
-                    ))
-
-    def kv_each(kind, act):
-        for step in range(heads):
-            h = turn(step)
-            owner = owner_of(h)
+                        q_sem.at[0], q_sem.at[1], at_core(owner, which),
+                    ).start()
+        else:
             which = jnp.where(owner == me, 1 - core, lane)
             relayed = jnp.where(which == lane, 0, 1)
             place = lane * line + lax.rem(spot - owner // pair + line, line)
-            act(remote(
-                stage.at[1 + kind, h], kv.at[kind, place], kv_send.at[0],
-                kv_recv.at[kind, relayed], at_core(owner, which),
-            ))
+            remote(
+                stage.at[kind, h], kv[kind - 1].at[place], kv_send.at[0],
+                kv_recv.at[jnp.where(relayed == 1, kind - 1, 2 if kind == 1 else 3 + place - lane * line)],
+                at_core(owner, which),
+            ).start()
+
+    turns = [(kind, step) for step in range(heads) for kind in range(3)]
+
+    def send_ready(kind):
+        now = [t for t in turns if t[0] <= kind]
+        for t in now:
+            turns.remove(t)
+            send(*t)
 
     value = whole(0)
     for h in range(heads):
         stage[0, h] = scaled(value[:, head_at(h)], gains[0], 1.0 / math.sqrt(head_size))
     meet()
-    q_each(lambda copy: copy.start())
+    send_ready(0)
     value = whole(1)
     for h in range(heads):
         stage[1, h] = scaled(value[:, head_at(h)], gains[1], 1.0)
-    kv_each(0, lambda copy: copy.start())
+    send_ready(1)
     value = whole(2)
     for h in range(heads):
         stage[2, h] = value[:, head_at(h)].astype(BF16)
-    kv_each(1, lambda copy: copy.start())
+    send_ready(2)
+
+    w_copy(sibling, pl.ds(0, inner), 1, 2).start()
 
     @pl.loop(0, line)
     def _(step):
         swap_copy(step).start()
 
     oldest = head_ref[0]
+    loads[5].wait()
+    gates[me] = dot(emb, ada[2])[0:1]
     for index, slot in enumerate(others):
         held = wout.at[slot, own_third]
         landed(held, w_recv.at[4 + index])
@@ -289,22 +303,34 @@
     def rank_of(block):
         return lax.rem(block - oldest + n, n)
 
-    def column_landed(kind, relayed, column):
-        base = column * line
-
+    def column_landed(kind, sem, column):
         @pl.when(local & (column == lane))
         def _():
-            landed(kv.at[kind, 0 : line - 1], kv_recv.at[kind, relayed])
+            landed(kv[kind].at[0 : line - 1], kv_recv.at[sem])
 
         @pl.when(jnp.logical_not(local & (column == lane)))
         def _():
-            landed(kv.at[kind, 0:line], kv_recv.at[kind, relayed])
+            landed(kv[kind].at[0:line], kv_recv.at[sem])
 
     def relay(kind, skip):
-        held = kv.at[kind, pl.ds(core * line + skip, line - skip)]
-        return remote(
-            held, held, relay_send.at[0], kv_recv.at[kind, 1], {"tensor": sibling}
-        )
+        held = kv[kind].at[pl.ds(core * line + skip, line - skip)]
+        return remote(held, held, relay_send.at[0], kv_recv.at[kind], {"tensor": sibling})
+
+    def values_landed():
+        @pl.loop(0, line)
+        def _(place):
+            held = values.at[core * line + place]
+            inside = (place == 0) & (core == lane)
+
+            @pl.when(jnp.logical_not(inside & local))
+            def _():
+                landed(held, kv_recv.at[3 + place])
+
+            @pl.when(jnp.logical_not(inside))
+            def _():
+                remote(
+                    held, held, relay_send.at[0], kv_recv.at[1], {"tensor": sibling}
+                ).start()
 
     def relay_on(kind):
         @pl.when(core == lane)
@@ -325,13 +351,14 @@
         )
 
     span = min(line, 4)
+    simple = line == span
 
     def absorb(column, base, count, fresh):
         def some(base, start, fresh):
             at = pl.ds(base, count)
             where = pl.ds(column * line + start, span)
             q = queries[at].reshape(count * half, head_size)
-            scores = dot_t(q, kv[0, where].reshape(span * rows, head_size))
+            scores = dot_t(q, keys[where].reshape(span * rows, head_size))
             ranks = [
                 rank_of(lax.rem(spot + start + index, line) * pair + column)
                 for index in range(span)
@@ -350,19 +377,45 @@
                 totals[base + block] = total if fresh else totals[base + block] + total
                 joined.append(jnp.concatenate([w.astype(BF16) for w in each], axis=1))
             product = dot(
-                jnp.concatenate(joined, axis=0), kv[1, where].reshape(span * rows, head_size)
+                jnp.concatenate(joined, axis=0), values[where].reshape(span * rows, head_size)
             ).reshape(count, half, head_size)
             acc[at] = product if fresh else acc[at] + product
 
-        if line == span:
-            some(base, 0, fresh)
-        else:
-            pl.loop(0, line // span)(lambda index: some(base, index * span, False))
+        pl.loop(0, line // span)(lambda index: some(base, index * span, False))
+
+    def score(column):
+        where = pl.ds(column * line, line)
+        q = queries[...].reshape(n * half, head_size)
+        scores = dot_t(q, keys[where].reshape(line * rows, head_size))
+        ranks = [
+            rank_of(lax.rem(spot + index, line) * pair + column) for index in range(line)
+        ]
+        for block in range(n):
+            rank = rank_of(block)
+            each = [
+                jnp.exp(
+                    scores[block * half : (block + 1) * half, index * rows : (index + 1) * rows]
+                    + jnp.where(ranks[index] <= rank, 0.0, -1e30)
+                )
+                for index in range(line)
+            ]
+            total = functools.reduce(jnp.add, each)
+            opening = column is core
+            totals[block] = total if opening else totals[block] + total
+            seen[1 - int(opening), block] = jnp.concatenate(
+                [w.astype(BF16) for w in each], axis=1
+            )
+
+    def product(which, column, at, count):
+        value = values[pl.ds(column * line, line)].reshape(line * rows, head_size)
+        return dot(
+            seen[which, at].reshape(count * half, line * rows), value
+        ).reshape(count, half, head_size)
 
 
     @pl.when(active)
     def _():
-        if line != span:
+        if not simple:
             acc[...] = jnp.zeros_like(acc)
             totals[...] = jnp.zeros_like(totals)
 
@@ -370,29 +423,34 @@
         def _():
             queries[me] = stage[0, own_head, pl.ds(pl.multiple_of(core * half, half), half)]
             for kind in range(2):
-                kv[kind, lane * line] = stage[1 + kind, own_head]
+                kv[kind][lane * line] = stage[1 + kind, own_head]
             landed(queries.at[0 : n - 1], q_sem.at[1])
 
         @pl.when(jnp.logical_not(local))
         def _():
             landed(queries, q_sem.at[1])
 
-        column_landed(0, 0, core)
+        column_landed(0, 2, core)
         relay_on(0)
-        column_landed(1, 0, core)
-        relay_on(1)
+        other = 1 - core
+        if simple:
+            score(core)
+        column_landed(0, 0, other)
+        if simple:
+            score(other)
+        place = lax.rem(oldest, pair) * line + lax.rem(oldest // pair - spot + line, line)
+        weights = jnp.exp(dot_t(queries[oldest], keys[place]))
+        weight_sum = jnp.sum(weights, axis=-1, keepdims=True)
+        values_landed()
         blocks = min(n, 8)
-        if n == blocks:
-            absorb(core, 0, n, True)
+        if simple:
+            acc[...] = product(0, core, slice(None), n)
         else:
             pl.loop(0, n // blocks)(lambda index: absorb(core, index * blocks, blocks, False))
-        column_landed(0, 1, 1 - core)
-        column_landed(1, 1, 1 - core)
-
-        place = lax.rem(oldest, pair) * line + lax.rem(oldest // pair - spot + line, line)
-        weights = jnp.exp(dot_t(queries[oldest], kv[0, place]))
-        lead = dot(weights.astype(BF16), kv[1, place])
-        lead = (lead / jnp.sum(weights, axis=-1, keepdims=True)).astype(BF16)
+        column_landed(1, 1, other)
+
+        lead = dot(weights.astype(BF16), values[place])
+        lead = (lead / weight_sum).astype(BF16)
 
         def slab_fill(block):
             at = lax.rem(slab_of(block), half)
@@ -411,11 +469,16 @@
 
         def last(step):
             base = batch_at(step)
-            absorb(1 - core, base, batch, False)
+            at = pl.ds(base, batch)
+            if simple:
+                value = acc[at] + product(1, other, at, batch)
+            else:
+                absorb(other, base, batch, False)
+                value = acc[at]
             for index in range(batch):
                 block = base + index
                 total = jnp.sum(totals[block], axis=-1, keepdims=True)
-                result[block, 0:half] = (acc[block] / total).astype(BF16)
+                result[block, 0:half] = (value[index] / total).astype(BF16)
                 slab_fill(block)
             for index in range(batch):
                 target = base + index
@@ -431,31 +494,6 @@
             pl.loop(0, n // batch)(last)
         attended[slot_at, own_head, own_piece] = result[me]
 
-    landed(lat_rows, row_sem.at[1])
-    swapped = jnp.full((slab, columns), buddy, jnp.int32) == oldest
-    for step in range(line):
-        target = step * pair + lane
-        kept = lat[pl.ds(slab_of(target), slab), pl.ds(first_column, columns)]
-        mixed_rows[step] = jnp.where(swapped, lat_rows[step], kept)
-    clean_rows_ref[spot] = mixed_rows[spot]
-
-    def row_copy(target_spot):
-        return remote(
-            mixed_rows.at[target_spot], clean_rows_ref.at[spot], row_sem.at[2], row_sem.at[3],
-            {"seq": target_spot * pair + lane},
-        )
-
-    @pl.loop(1, line)
-    def _(step):
-        row_copy(lax.rem(spot + step, line)).start()
-
-    loads[5].wait()
-    gates[me] = dot(emb, ada[2])[0:1]
-
-    @pl.loop(1, n)
-    def _(step):
-        gate_copy(lax.rem(me + step, n)).start()
-
     def region(slot, h):
         return attended.at[slot, h, own_piece]
 
@@ -476,20 +514,73 @@
         g = jnp.where(me < n // 2, owners - 1 - step, step)
         return g, plane * pair + lax.rem(g, pair), g // pair
 
+    def row_copy(target_spot):
+        return remote(
+            mixed_rows.at[target_spot], clean_rows_ref.at[spot], row_sem.at[2], row_sem.at[3],
+            {"seq": target_spot * pair + lane},
+        )
+
+    def share_rows():
+        landed(lat_rows, row_sem.at[1])
+        swapped = jnp.full((slab, columns), buddy, jnp.int32) == oldest
+        for step in range(line):
+            target = step * pair + lane
+            kept = lat[pl.ds(slab_of(target), slab), pl.ds(first_column, columns)]
+            mixed_rows[step] = jnp.where(swapped, lat_rows[step], kept)
+        clean_rows_ref[spot] = mixed_rows[spot]
+
+
+        @pl.loop(1, line)
+        def _(step):
+            row_copy(lax.rem(spot + step, line)).start()
+
+        @pl.loop(1, n)
+        def _(step):
+            gate_copy(lax.rem(me + step, n)).start()
+
+
+    @pl.when(active)
+    def _():
+        for way in range(1, planes):
+            across(slot_at, own_head, mine, way).start()
+        to_sibling(slot_at, own_head, 0).start()
+
+    share_rows()
     for step in range(owners):
         g, slot, h = ordered(step)
 
         @pl.when(first + g != me)
         def _():
             landed(region(slot, h), direct_recv.at[g])
-
+            for way in range(1, planes):
+                across(slot, h, g, way).start()
+            to_sibling(slot, h, 0).start()
+
+    def plane_dot(base, span):
+        joined = jnp.concatenate(
+            [attended[base + which, h, span] for which in range(pair) for h in range(heads)],
+            axis=1,
+        )
+        weights = wout[pl.ds(base, pair)].reshape(pair * inner, columns)
+        return dot(joined, weights)
+
+    def finish(which):
+        start = pl.multiple_of(which * piece, 16)
+        total = partial[pl.ds(start, piece), :]
         for way in range(1, planes):
-            across(slot, h, g, way).start()
-        to_sibling(slot, h, 0).start()
-
-    def slot_dot(slot):
-        joined = jnp.concatenate([attended[slot, h] for h in range(heads)], axis=1)
-        return dot(joined, wout[slot])
+            base = lax.rem(plane + way, planes) * pair
+            total = total + plane_dot(base, pl.ds(start, piece))
+        at = pl.ds(pl.multiple_of(which * half, half), half)
+        states = lat[at, pl.ds(first_column, columns)].astype(F32)
+        updated = (states + gates[me] * total[0:half]).astype(BF16)
+        leaving = jnp.full((half, columns), rank_of(me), jnp.int32) == 0
+        updated_ref[at, :] = jnp.where(leaving, noise[at, :], updated)
+
+        @pl.when(own_slab // half == which)
+        def _():
+            updated_ref[rows:, :] = (
+                clean_rows_ref[oldest // pair].astype(F32) + gates[oldest] * total[half:]
+            ).astype(BF16)
 
     for way in range(1, planes):
         for step in range(owners):
@@ -501,27 +592,15 @@
     loads[8].wait()
     landed(wout.at[0], w_recv.at[2])
     landed(attended.at[0:pair, :, 0:piece], sib_recv.at[0])
-    total = slot_dot(part) + slot_dot(sibling)
+    partial[...] = plane_dot(plane * pair, slice(None))
     landed(wout.at[0 : parts - pair, always], w_recv.at[1])
     landed(wout.at[0 : parts - pair, 0:third], w_recv.at[3])
-    landed(attended.at[0 : parts - pair, :, 0:piece], sib_recv.at[1])
-    for slot in others:
-        total = total + slot_dot(slot)
-
     landed(gates.at[0 : n - 1], gate_sem.at[1])
     landed(lat_rows.at[0 : line - 1], row_sem.at[3])
     loads[9].wait()
-    own_rank = rank_of(me)
-    own_states = lat[:, pl.ds(first_column, columns)].astype(F32)
-    mixed = jnp.concatenate([total[0:half], total[piece : piece + half]], axis=0)
-    updated = (own_states + gates[me] * mixed).astype(BF16)
-    leaving = jnp.full((rows, columns), own_rank, jnp.int32) == 0
-    updated_ref[0:rows, :] = jnp.where(leaving, noise[...], updated)
-    upper = jnp.full((slab, columns), own_slab, jnp.int32) >= half
-    clean = jnp.where(upper, total[piece + half :], total[half:piece])
-    updated_ref[rows:, :] = (
-        clean_rows_ref[oldest // pair].astype(F32) + gates[oldest] * clean
-    ).astype(BF16)
+    finish(core)
+    landed(attended.at[0 : parts - pair, :, 0:piece], sib_recv.at[1])
+    finish(1 - core)
 
     sent(mods.at[0 : parts - 1], mod_send.at[0])
 
@@ -533,7 +612,7 @@
     def _():
         sent(queries.at[0:owners], q_sem.at[0])
 
-    sent(kv.at[:, 0:heads], kv_send.at[0])
+    sent(keys.at[0 : pair * heads], kv_send.at[0])
     sent(gates.at[0 : n - 1], gate_sem.at[0])
     sent(lat_rows, row_sem.at[0])
     sent(lat_rows.at[0 : line - 1], row_sem.at[2])
@@ -549,11 +628,11 @@
 
         @pl.when(core == lane)
         def _():
-            sent(kv.at[:, 0 : line - 1], relay_send.at[0])
+            sent(keys.at[0 : pair * (line - 1)], relay_send.at[0])
 
         @pl.when(core != lane)
         def _():
-            sent(kv.at[:, 0:line], relay_send.at[0])
+            sent(keys, relay_send.at[0])
 
 
 def finish_kernel(updated_ref, window_ref, clean_ref):
@@ -603,13 +682,16 @@
             pltpu.VMEM((3, rows, inner), F32),
             pltpu.VMEM((3, heads, rows, head_size), BF16),
             pltpu.VMEM((n, half, head_size), BF16),
-            pltpu.VMEM((2, n, rows, head_size), BF16),
+            pltpu.VMEM((n, rows, head_size), BF16),
+            pltpu.VMEM((n, rows, head_size), BF16),
             pltpu.VMEM((n, half, head_size), F32),
             pltpu.VMEM((n, half, rows), F32),
+            pltpu.VMEM((2, n if n <= 8 else 1, half, n // 2 * rows), BF16),
             pltpu.VMEM((n, half + slab, head_size), BF16),
             pltpu.VMEM((parts, heads, 2 * (half + slab), head_size), BF16),
+            pltpu.VMEM((2 * (half + slab), columns), F32),
             pltpu.SemaphoreType.REGULAR, dma((10,)), dma((1,)), dma((2,)), dma((2,)), dma((4,)), dma((3,)), dma((4 + parts - 2,)),
-            dma((2,)), dma((1,)), dma((2, 2)), dma((1,)), dma((1,)), dma((owners,)),
+            dma((2,)), dma((1,)), dma((3 + n // 2,)), dma((1,)), dma((1,)), dma((owners,)),
             dma((parts // 2 - 1, owners)), dma((2,)), dma((2,)),
         ],
         compiler_params=pltpu.CompilerParams(

time: 30.6 us -> 30.4 us (level)
  Pallas kernels: 28.4 us -> 28 us
    pallas_call x1, Pallas kernels: 27.8 us -> 27.4 us  [local(): pl.pallas_call(functools.partial(kernel, n, parts, slab, clean_rows), out...]
where the time goes in v4:
time: 30.4 us; the launch traced here: 30 us
  Pallas kernels  28 us (92%)
  between operations  1.93 us (6%)
    pallas_call x1, Pallas kernels, local(): pl.pallas_call(functools.partial(kernel, n, parts, slab, clean_rows), out...  27.4 us
    pallas_call x1, Pallas kernels, local(): pl.pallas_call(finish_kernel, out_shape=(jax.ShapeDtypeStruct((rows, colu...  0.68 us

profile of v4, /device:TPU:1, one launch (start us, length us, event | category | flops | bytes accessed | tf_op | source)
XLA Modules:
  0.0 30.0 jit_solution(16354367465343156548)
XLA Ops:
  1.9 27.4 %shard_map.104.updated_ref = bf16[144,640]{1,0:T(8,128)(2,1)S(1)} custom-call(s32[1]{0:T(128)S(6)} %copy.12.head_ref, s32[1]{0:T(128)S(6)} %copy.11.level_ref, f32[1,128]{1,0:T(1,128)} %bitcast.8, f32[1,128]{1,0:T(1,128)} %bitcast.9, bf16[128,640]{1,0:T(8,128)(2,1)} %noise_hbm.1, bf16[128,2560]{1,0:T(8,128)(2,1)} %lat_hbm.1, bf16[3,256,640]{2,1,0:T(8,128)(2,1)} %bitcast.7, ...), custom_call_target="tpu_custom_call" | custom-call | tf_op jit(solution)/shard_map/pallas_call | solution.py:662
  29.3 0.7 %shard_map.105 = (bf16[128,640]{1,0:T(8,128)(2,1)}, bf16[16,640]{1,0:T(8,128)(2,1)}) custom-call(bf16[144,640]{1,0:T(8,128)(2,1)S(1)} %shard_map.104.updated_ref), custom_call_target="tpu_custom_call" | custom-call | tf_op jit(solution)/shard_map/pallas_call | solution.py:706

commit v5 on v4

--- a/solution.py
+++ b/solution.py
@@ -264,27 +264,23 @@
                 at_core(owner, which),
             ).start()
 
-    turns = [(kind, step) for step in range(heads) for kind in range(3)]
-
-    def send_ready(kind):
-        now = [t for t in turns if t[0] <= kind]
-        for t in now:
-            turns.remove(t)
-            send(*t)
-
+    def send_all(kind):
+        for step in range(heads):
+            send(kind, step)
+
+    value = whole(2)
+    for h in range(heads):
+        stage[2, h] = value[:, head_at(h)].astype(BF16)
+    meet()
+    send_all(2)
+    value = whole(1)
+    for h in range(heads):
+        stage[1, h] = scaled(value[:, head_at(h)], gains[1], 1.0)
+    send_all(1)
     value = whole(0)
     for h in range(heads):
         stage[0, h] = scaled(value[:, head_at(h)], gains[0], 1.0 / math.sqrt(head_size))
-    meet()
-    send_ready(0)
-    value = whole(1)
-    for h in range(heads):
-        stage[1, h] = scaled(value[:, head_at(h)], gains[1], 1.0)
-    send_ready(1)
-    value = whole(2)
-    for h in range(heads):
-        stage[2, h] = value[:, head_at(h)].astype(BF16)
-    send_ready(2)
+    send_all(0)
 
     w_copy(sibling, pl.ds(0, inner), 1, 2).start()
 
@@ -383,15 +379,15 @@
 
         pl.loop(0, line // span)(lambda index: some(base, index * span, False))
 
-    def score(column):
+    def score(column, base, count):
         where = pl.ds(column * line, line)
-        q = queries[...].reshape(n * half, head_size)
+        q = queries[pl.ds(base, count)].reshape(count * half, head_size)
         scores = dot_t(q, keys[where].reshape(line * rows, head_size))
         ranks = [
             rank_of(lax.rem(spot + index, line) * pair + column) for index in range(line)
         ]
-        for block in range(n):
-            rank = rank_of(block)
+        for block in range(count):
+            rank = rank_of(base + block)
             each = [
                 jnp.exp(
                     scores[block * half : (block + 1) * half, index * rows : (index + 1) * rows]
@@ -401,8 +397,8 @@
             ]
             total = functools.reduce(jnp.add, each)
             opening = column is core
-            totals[block] = total if opening else totals[block] + total
-            seen[1 - int(opening), block] = jnp.concatenate(
+            totals[base + block] = total if opening else totals[base + block] + total
+            seen[1 - int(opening), base + block] = jnp.concatenate(
                 [w.astype(BF16) for w in each], axis=1
             )
 
@@ -424,30 +420,28 @@
             queries[me] = stage[0, own_head, pl.ds(pl.multiple_of(core * half, half), half)]
             for kind in range(2):
                 kv[kind][lane * line] = stage[1 + kind, own_head]
-            landed(queries.at[0 : n - 1], q_sem.at[1])
-
-        @pl.when(jnp.logical_not(local))
-        def _():
-            landed(queries, q_sem.at[1])
-
+
+        other = 1 - core
+        values_landed()
         column_landed(0, 2, core)
         relay_on(0)
-        other = 1 - core
-        if simple:
-            score(core)
         column_landed(0, 0, other)
-        if simple:
-            score(other)
+        column_landed(1, 1, other)
+
+        @pl.when(local)
+        def _():
+            landed(queries.at[0 : n - 1], q_sem.at[1])
+
+        @pl.when(jnp.logical_not(local))
+        def _():
+            landed(queries, q_sem.at[1])
+
         place = lax.rem(oldest, pair) * line + lax.rem(oldest // pair - spot + line, line)
         weights = jnp.exp(dot_t(queries[oldest], keys[place]))
         weight_sum = jnp.sum(weights, axis=-1, keepdims=True)
-        values_landed()
         blocks = min(n, 8)
-        if simple:
-            acc[...] = product(0, core, slice(None), n)
-        else:
+        if not simple:
             pl.loop(0, n // blocks)(lambda index: absorb(core, index * blocks, blocks, False))
-        column_landed(1, 1, other)
 
         lead = dot(weights.astype(BF16), values[place])
         lead = (lead / weight_sum).astype(BF16)
@@ -471,7 +465,9 @@
             base = batch_at(step)
             at = pl.ds(base, batch)
             if simple:
-                value = acc[at] + product(1, other, at, batch)
+                score(core, base, batch)
+                score(other, base, batch)
+                value = product(0, core, at, batch) + product(1, other, at, batch)
             else:
                 absorb(other, base, batch, False)
                 value = acc[at]

time: 30.4 us -> 29.8 us (0.980)
  Pallas kernels: 28 us -> 27.6 us
    pallas_call x1, Pallas kernels: 27.4 us -> 26.9 us  [local(): pl.pallas_call(functools.partial(kernel, n, parts, slab, clean_rows), out...]
where the time goes in v5:
time: 29.8 us; the launch traced here: 29.5 us
  Pallas kernels  27.6 us (93%)
  between operations  1.93 us (6%)
    pallas_call x1, Pallas kernels, local(): pl.pallas_call(functools.partial(kernel, n, parts, slab, clean_rows), out...  26.9 us
    pallas_call x1, Pallas kernels, local(): pl.pallas_call(finish_kernel, out_shape=(jax.ShapeDtypeStruct((rows, colu...  0.68 us

profile of v5, /device:TPU:1, one launch (start us, length us, event | category | flops | bytes accessed | tf_op | source)
XLA Modules:
  0.0 29.5 jit_solution(16165029226620104331)
XLA Ops:
  1.9 26.9 %shard_map.104.updated_ref = bf16[144,640]{1,0:T(8,128)(2,1)S(1)} custom-call(s32[1]{0:T(128)S(6)} %copy.12.head_ref, s32[1]{0:T(128)S(6)} %copy.11.level_ref, f32[1,128]{1,0:T(1,128)} %bitcast.8, f32[1,128]{1,0:T(1,128)} %bitcast.9, bf16[128,640]{1,0:T(8,128)(2,1)} %noise_hbm.1, bf16[128,2560]{1,0:T(8,128)(2,1)} %lat_hbm.1, bf16[3,256,640]{2,1,0:T(8,128)(2,1)} %bitcast.7, ...), custom_call_target="tpu_custom_call" | custom-call | tf_op jit(solution)/shard_map/pallas_call | solution.py:658
  28.8 0.7 %shard_map.105 = (bf16[128,640]{1,0:T(8,128)(2,1)}, bf16[16,640]{1,0:T(8,128)(2,1)}) custom-call(bf16[144,640]{1,0:T(8,128)(2,1)S(1)} %shard_map.104.updated_ref), custom_call_target="tpu_custom_call" | custom-call | tf_op jit(solution)/shard_map/pallas_call | solution.py:702
